TPU v7x, 128 devices: a whole 4x4x4 slice. The times are simulated.
128 devices in a mesh: patch: 8 (over y, x_lo), hid: 16 (over x_hi, z, core).
Axes of the slice: x: 4 (x_hi: 2, x_lo: 2; x = x_hi * 2 + x_lo), y: 4, z: 4, core: 2. Of those that a mesh axis runs over, the one named last changes fastest.
Arguments:
- frames: bfloat16 [4, 2, 32, 64, 512], P(None, None, 'patch', None, 'hid'), may hold values from -6 to 6
- hidden_start: bfloat16 [2, 32, 64, 512], P(None, 'patch', None, 'hid'), may hold values from -4 to 4
- cell_start: float32 [2, 32, 64, 512], P(None, 'patch', None, 'hid'), may hold values from -6 to 6
- input_weight: bfloat16 [3, 3, 512, 4, 512], P(None, None, None, None, 'hid'), may hold values from -0.09375 to 0.09375
- hidden_weight: bfloat16 [3, 3, 512, 4, 512], P(None, None, None, None, 'hid'), may hold values from -0.09375 to 0.09375
- gate_bias: float32 [4, 512], P(None, 'hid'), may hold values from -3 to 3
- first_weight: bfloat16 [3, 3, 512, 512], replicated, may hold values from -0.09375 to 0.09375
- first_bias: float32 [512], replicated, may hold values from -3 to 3
- second_weight: bfloat16 [3, 3, 512, 512], replicated, may hold values from -0.09375 to 0.09375
- second_bias: float32 [512], replicated, may hold values from -3 to 3
Outputs:
- decoded: bfloat16 [2, 32, 64, 512], P(None, 'patch', 'hid')
- cell_final: float32 [2, 32, 64, 512], P(None, 'patch', None, 'hid')
All inputs are finite; a program needn't handle non-finite values.
Results may differ from a plain program's by a relative error of at most 0.0045.
Values may be sent and summed in bfloat16 or wider, within the bound.
A program may use at most 128 MiB of HBM per device.

v0:
```python
import jax
import jax.numpy as jnp
from jax import lax
from jax.sharding import PartitionSpec as P

STEPS = 4


FORGET_BIAS = 1.0


def extended_2(block, sides, width):
    for axis, dim in sides:
        count = lax.axis_size(axis)
        forward = [(i, i + 1) for i in range(count - 1)]
        backward = [(target, source) for source, target in forward]
        low = lax.ppermute(
            lax.slice_in_dim(block, block.shape[dim] - width, None, axis=dim), axis, forward
        )
        high = lax.ppermute(lax.slice_in_dim(block, 0, width, axis=dim), axis, backward)
        block = jnp.concatenate([low, block, high], axis=dim)
    return block


def conv_taps(padded, weight):
    batch_count, padded_rows, padded_cols, channel_count = padded.shape
    row_count = padded_rows - 2
    col_count = padded_cols - 2
    summed = jnp.zeros((batch_count * row_count * col_count, weight.shape[-1]), jnp.float32)
    for tap_row in range(3):
        for tap_col in range(3):
            window = padded[:, tap_row : tap_row + row_count, tap_col : tap_col + col_count, :]
            summed = summed + jnp.dot(
                window.reshape(-1, channel_count),
                weight[tap_row, tap_col],
                preferred_element_type=jnp.float32,
            )
    return summed.reshape(batch_count, row_count, col_count, weight.shape[-1])


def lstm_update(gates, cell):
    shaped = gates.reshape(gates.shape[:-1] + (4, gates.shape[-1] // 4))
    input_gate = jax.nn.sigmoid(shaped[..., 0, :])
    forget_gate = jax.nn.sigmoid(shaped[..., 1, :] + FORGET_BIAS)
    candidate = jnp.tanh(shaped[..., 2, :])
    output_gate = jax.nn.sigmoid(shaped[..., 3, :])
    cell = forget_gate * cell + input_gate * candidate
    hidden = (output_gate * jnp.tanh(cell)).astype(jnp.bfloat16)
    return (hidden, cell)


def pad_columns(image):
    return jnp.pad(image, ((0, 0), (0, 0), (1, 1), (0, 0)))


def per_device(
    frames,
    hidden_start,
    cell_start,
    input_weight,
    hidden_weight,
    gate_bias,
    first_weight,
    first_bias,
    second_weight,
    second_bias,
):
    local_gates = 4 * input_weight.shape[-1]
    wide_input = input_weight.reshape(3, 3, input_weight.shape[2], local_gates)
    wide_hidden = hidden_weight.reshape(3, 3, hidden_weight.shape[2], local_gates)
    bias_row = gate_bias.reshape(-1)
    all_frames = lax.all_gather(frames, "hid", axis=4, tiled=True)
    framed = extended_2(all_frames, (("patch", 2),), 1)
    hidden = hidden_start
    cell = cell_start
    for time_index in range(STEPS):
        edged = extended_2(hidden, (("patch", 1),), 1)
        rimmed = lax.all_gather(edged, "hid", axis=3, tiled=True)
        gates = (
            conv_taps(pad_columns(framed[time_index]), wide_input)
            + conv_taps(pad_columns(rimmed), wide_hidden)
            + bias_row
        )
        hidden, cell = lstm_update(gates, cell)
    tiled = lax.all_to_all(hidden, "hid", split_axis=2, concat_axis=3, tiled=True)
    outer = extended_2(tiled, (("patch", 1), ("hid", 2)), 2)
    extended = jax.nn.silu(conv_taps(outer, first_weight) + first_bias)
    tile_rows = tiled.shape[1]
    tile_cols = tiled.shape[2]
    row_place = lax.axis_index("patch") * tile_rows + jnp.arange(tile_rows + 2, dtype=jnp.int32) - 1
    col_place = lax.axis_index("hid") * tile_cols + jnp.arange(tile_cols + 2, dtype=jnp.int32) - 1
    row_inside = (row_place >= 0) & (row_place < tile_rows * lax.axis_size("patch"))
    col_inside = (col_place >= 0) & (col_place < tile_cols * lax.axis_size("hid"))
    inside = row_inside[:, None] & col_inside[None, :]
    middle_rimmed = jnp.where(inside[None, :, :, None], extended, 0.0).astype(jnp.bfloat16)
    decoded = (conv_taps(middle_rimmed, second_weight) + second_bias).astype(jnp.bfloat16)
    return (decoded, cell)


def solution(mesh):
    return jax.shard_map(
        per_device,
        mesh=mesh,
        in_specs=(
            P(None, None, "patch", None, "hid"),
            P(None, "patch", None, "hid"),
            P(None, "patch", None, "hid"),
            P(None, None, None, None, "hid"),
            P(None, None, None, None, "hid"),
            P(None, "hid"),
            P(),
            P(),
            P(),
            P(),
        ),
        out_specs=(P(None, "patch", "hid", None), P(None, "patch", None, "hid")),
        check_vma=False,
    )
```

profile of v0, /device:TPU:11, one launch (start us, length us, event | category | flops | bytes accessed | tf_op | source)
XLA Modules:
  0.0 330.5 jit_solution(6967375789066192866)
XLA Ops:
  10.0 3.2 collective-permute-start.2
  15.3 3.3 collective-permute-done.3
  18.7 31.2 %all_gather.16 = bf16[2,6,64,512]{2,0,1,3:T(2,128)(2,1)S(1)} all-gather(bf16[2,6,64,32]{2,0,1,3:T(2,128)(2,1)S(1)} %pad_maximum_fusion.7), channel_id=1, replica_groups=mesh['patch'=8,'hid'=16] {'hid'}, dimensions={3}, use_global_device_ids=true | all-gather | bytes 835584 | tf_op jit(solution)/shard_map/all_gather | solution.py:78
  55.5 14.9 %all-gather.2.cloned.1.call-done = bf16[4,2,4,64,512]{3,2,1,0,4:T(4,128)(2,1)} async-done(((bf16[4,2,4,64,32]{3,2,1,0,4:T(4,128)(2,1)}), bf16[4,2,4,64,512]{3,2,1,0,4:T(4,128)(2,1)}) %all-gather.2.cloned.1.call-update) | async-done | bytes 2097168 | tf_op jit(solution)/shard_map/all_gather | solution.py:72
  70.4 5.6 %copy.91 = bf16[4,2,4,64,512]{4,3,2,1,0:T(8,128)(2,1)S(1)} copy(bf16[4,2,4,64,512]{3,2,1,0,4:T(4,128)(2,1)} %all-gather.2.cloned.1.call-done) | data formatting | bytes 4194304 | tf_op jit(solution)/shard_map/all_gather | solution.py:72
  76.1 4.1 %collective-permute-start = (bf16[4,2,1,64,512]{4,3,2,1,0:T(8,128)(2,1)S(1)}, bf16[4,2,1,64,512]{4,3,2,1,0:T(8,128)(2,1)S(1)}, u32[]{:S(2)}, u32[]{:S(2)}) collective-permute-start(bf16[4,2,1,64,512]{4,3,2,1,0:T(8,128)(2,1)S(1)} %get-tuple-element.20), channel_id=1, source_target_pairs={{0,16},{16,32},{32,48},{48,64},{64,80},{80,96},{96,112},{1,17},{17... | collective-permute-start | bytes 1572872 | tf_op jit(solution)/shard_map/ppermute | solution.py:17
  83.5 7.9 %collective-permute-done = bf16[4,2,1,64,512]{4,3,2,1,0:T(8,128)(2,1)S(1)} collective-permute-done((bf16[4,2,1,64,512]{4,3,2,1,0:T(8,128)(2,1)S(1)}, bf16[4,2,1,64,512]{4,3,2,1,0:T(8,128)(2,1)S(1)}, u32[]{:S(2)}, u32[]{:S(2)}) %collective-permute-start) | collective-permute-done | bytes 524320 | tf_op jit(solution)/shard_map/ppermute | solution.py:17
  91.4 12.2 %collective-permute-done.1 = bf16[4,2,1,64,512]{4,3,2,1,0:T(8,128)(2,1)S(1)} collective-permute-done((bf16[4,2,1,64,512]{4,3,2,1,0:T(8,128)(2,1)S(1)}, bf16[4,2,1,64,512]{4,3,2,1,0:T(8,128)(2,1)S(1)}, u32[]{:S(2)}, u32[]{:S(2)}) %collective-permute-start.1) | collective-permute-done | bytes 524320 | tf_op jit(solution)/shard_map/ppermute | solution.py:20
  104.3 4.7 %pad_slice_fusion.36 = (bf16[2,4,64,512]{3,2,1,0:T(8,128)(2,1)}, bf16[2,4,64,512]{3,2,1,0:T(8,128)(2,1)}, bf16[2,4,64,512]{3,2,1,0:T(8,128)(2,1)}, bf16[2,4,64,5...) fusion(bf16[2,6,64,512]{3,2,1,0:T(8,128)(2,1)S(1)} %get-tuple-e, ...), kind=kLoop, calls=%fused_computation.125 | loop fusion | bytes 14155776 | tf_op jit(solution)/shard_map/slice | solution.py:32
  110.9 4.5 %pad_slice_fusion.24 = (bf16[2,4,64,512]{3,2,1,0:T(8,128)(2,1)S(1)}, bf16[2,4,64,512]{3,2,1,0:T(8,128)(2,1)S(1)}, bf16[2,4,64,512]{3,2,1,0:T(8,128)(2,1)S(1)}, b...) fusion(bf16[2,6,64,512]{3,2,1,0:T(8,128)(2,1)S(1)} %get-tuple-e, ...), kind=kLoop, calls=%fused_computation.113 | loop fusion | bytes 14155776 | tf_op jit(solution)/shard_map/slice | solution.py:32
  126.3 3.7 %collective-permute-start.4 = (bf16[2,1,64,32]{2,1,0,3:T(2,128)(2,1)S(1)}, bf16[2,1,64,32]{2,1,0,3:T(2,128)(2,1)S(1)}, u32[]{:S(2)}, u32[]{:S(2)}) collective-permute-start(bf16[2,1,64,32]{2,1,0,3:T(2,128)(2,1)S(1)} %get-tuple-element.121), channel_id=1, source_target_pairs={{0,16},{16,32},{32,48},{48,64},{64,80},{80,96},{96,112},{1,17},{17... | collective-permute-start | bytes 24584 | tf_op jit(solution)/shard_map/ppermute | solution.py:17
  143.0 27.7 %all_gather.17 = bf16[2,6,64,512]{2,0,1,3:T(2,128)(2,1)} all-gather(bf16[2,6,64,32]{2,0,1,3:T(2,128)(2,1)S(1)} %copy.103), channel_id=1, replica_groups=mesh['patch'=8,'hid'=16] {'hid'}, dimensions={3}, use_global_device_ids=true | all-gather | bytes 835584 | tf_op jit(solution)/shard_map/all_gather | solution.py:78
  170.7 3.5 %copy.104 = bf16[2,6,64,512]{3,2,1,0:T(8,128)(2,1)S(1)} copy(bf16[2,6,64,512]{2,0,1,3:T(2,128)(2,1)} %all_gather.17) | data formatting | bytes 1572864 | tf_op jit(solution)/shard_map/all_gather | solution.py:78
  180.1 3.7 %collective-permute-start.6 = (bf16[2,1,64,32]{2,1,0,3:T(2,128)(2,1)S(1)}, bf16[2,1,64,32]{2,1,0,3:T(2,128)(2,1)S(1)}, u32[]{:S(2)}, u32[]{:S(2)}) collective-permute-start(bf16[2,1,64,32]{2,1,0,3:T(2,128)(2,1)S(1)} %get-tuple-element.119), channel_id=1, source_target_pairs={{0,16},{16,32},{32,48},{48,64},{64,80},{80,96},{96,112},{1,17},{17... | collective-permute-start | bytes 24584 | tf_op jit(solution)/shard_map/ppermute | solution.py:17
  186.8 2.6 collective-permute-done.7
  189.7 27.0 %all_gather.18 = bf16[2,6,64,512]{2,0,1,3:T(2,128)(2,1)} all-gather(bf16[2,6,64,32]{2,0,1,3:T(2,128)(2,1)S(1)} %copy.109), channel_id=1, replica_groups=mesh['patch'=8,'hid'=16] {'hid'}, dimensions={3}, use_global_device_ids=true | all-gather | bytes 835584 | tf_op jit(solution)/shard_map/all_gather | solution.py:78
  216.7 3.5 %copy.110 = bf16[2,6,64,512]{3,2,1,0:T(8,128)(2,1)S(1)} copy(bf16[2,6,64,512]{2,0,1,3:T(2,128)(2,1)} %all_gather.18) | data formatting | bytes 1572864 | tf_op jit(solution)/shard_map/all_gather | solution.py:78
  227.7 3.4 %collective-permute-start.9 = (bf16[2,1,64,32]{2,1,0,3:T(2,128)(2,1)S(1)}, bf16[2,1,64,32]{2,1,0,3:T(2,128)(2,1)S(1)}, u32[]{:S(2)}, u32[]{:S(2)}) collective-permute-start(bf16[2,1,64,32]{2,1,0,3:T(2,128)(2,1)S(1)} %get-tuple-element.118), channel_id=1, source_target_pairs={{16,0},{32,16},{48,32},{64,48},{80,64},{96,80},{112,96},{17,1},{33... | collective-permute-start | bytes 24584 | tf_op jit(solution)/shard_map/ppermute | solution.py:20
  233.4 27.1 %all_gather.19 = bf16[2,6,64,512]{2,0,1,3:T(2,128)(2,1)} all-gather(bf16[2,6,64,32]{2,0,1,3:T(2,128)(2,1)S(1)} %copy.115), channel_id=1, replica_groups=mesh['patch'=8,'hid'=16] {'hid'}, dimensions={3}, use_global_device_ids=true | all-gather | bytes 835584 | tf_op jit(solution)/shard_map/all_gather | solution.py:78
  260.5 3.5 %copy.116 = bf16[2,6,64,512]{3,2,1,0:T(8,128)(2,1)S(1)} copy(bf16[2,6,64,512]{2,0,1,3:T(2,128)(2,1)} %all_gather.19) | data formatting | bytes 1572864 | tf_op jit(solution)/shard_map/all_gather | solution.py:78
  270.1 4.4 %all-to-all-start = ((bf16[16,2,512]{2,1,0:T(2,128)(2,1)}), bf16[16,2,512]{2,1,0:T(2,128)(2,1)S(1)}, u32[]{:S(2)}, u32[]{:S(2)}) async-start(bf16[16,2,512]{2,1,0:T(2,128)(2,1)} %reshape.550), calls=%async_computation | async-start | bytes 65536 | tf_op jit(solution)/shard_map/all_to_all | solution.py:85
  274.5 7.3 %all-to-all-done = bf16[16,2,512]{2,1,0:T(2,128)(2,1)S(1)} async-done(((bf16[16,2,512]{2,1,0:T(2,128)(2,1)}), bf16[16,2,512]{2,1,0:T(2,128)(2,1)S(1)}, u32[]{:S(2)}, u32[]{:S(2)}) %all-to-all-start) | async-done | bytes 32800 | tf_op jit(solution)/shard_map/all_to_all | solution.py:85
  284.8 2.7 collective-permute-start.11
  290.2 3.9 %collective-permute-start.12 = (bf16[2,8,2,512]{3,2,1,0:T(2,128)(2,1)S(1)}, bf16[2,8,2,512]{3,2,1,0:T(2,128)(2,1)S(1)}, u32[]{:S(2)}, u32[]{:S(2)}) collective-permute-start(bf16[2,8,2,512]{3,2,1,0:T(2,128)(2,1)S(1)} %get-tuple-element.115), channel_id=1, source_target_pairs={{0,1},{1,2},{2,3},{3,4},{4,5},{5,6},{6,7},{7,8},{8,9},{9,10},{10,1... | collective-permute-start | bytes 98312 | tf_op jit(solution)/shard_map/ppermute | solution.py:17
  (260 shorter events, 99.5 us)
Async XLA Ops:
  7.2 63.2 %all-gather.2.cloned.1.call-start = ((), (), s32[]{:S(2)}) async-start(), calls=%async_computation.1 | async-start | bytes 4456448 | tf_op jit(solution)/shard_map/all_gather | solution.py:72
  10.0 5.3 %collective-permute-start.2 = (bf16[2,1,64,32]{2,0,1,3:T(2,128)(2,1)S(1)}, bf16[2,1,64,32]{2,0,1,3:T(2,128)(2,1)S(1)}, u32[]{:S(2)}, u32[]{:S(2)}) collective-permute-start(bf16[2,1,64,32]{2,0,1,3:T(2,128)(2,1)S(1)} %get-tuple-element.123), channel_id=1, source_target_pairs={{0,16},{16,32},{32,48},{48,64},{64,80},{80,96},{96,112},{1,17},{17... | collective-permute-start | bytes 24584 | tf_op jit(solution)/shard_map/ppermute | solution.py:17
  13.2 5.4 %collective-permute-start.3 = (bf16[2,1,64,32]{2,0,1,3:T(2,128)(2,1)S(1)}, bf16[2,1,64,32]{2,0,1,3:T(2,128)(2,1)S(1)}, u32[]{:S(2)}, u32[]{:S(2)}) collective-permute-start(bf16[2,1,64,32]{2,0,1,3:T(2,128)(2,1)S(1)} %get-tuple-element.124), channel_id=1, source_target_pairs={{16,0},{32,16},{48,32},{64,48},{80,64},{96,80},{112,96},{17,1},{33... | collective-permute-start | bytes 24584 | tf_op jit(solution)/shard_map/ppermute | solution.py:20
  76.0 6.2 %copy-start.26 = (bf16[2,4,64,512]{3,2,1,0:T(8,128)(2,1)S(1)}, bf16[2,4,64,512]{3,2,1,0:T(8,128)(2,1)}, u32[]{:S(2)}) copy-start(bf16[2,4,64,512]{3,2,1,0:T(8,128)(2,1)} %get-tuple-element.89) | copy-start | bytes 1572868
  76.0 6.5 %copy-start.25 = (bf16[2,4,64,512]{3,2,1,0:T(8,128)(2,1)S(1)}, bf16[2,4,64,512]{3,2,1,0:T(8,128)(2,1)}, u32[]{:S(2)}) copy-start(bf16[2,4,64,512]{3,2,1,0:T(8,128)(2,1)} %get-tuple-element.90) | copy-start | bytes 1572868
  76.1 15.3 %collective-permute-start = (bf16[4,2,1,64,512]{4,3,2,1,0:T(8,128)(2,1)S(1)}, bf16[4,2,1,64,512]{4,3,2,1,0:T(8,128)(2,1)S(1)}, u32[]{:S(2)}, u32[]{:S(2)}) collective-permute-start(bf16[4,2,1,64,512]{4,3,2,1,0:T(8,128)(2,1)S(1)} %get-tuple-element.20), channel_id=1, source_target_pairs={{0,16},{16,32},{32,48},{48,64},{64,80},{80,96},{96,112},{1,17},{17... | collective-permute-start | bytes 1572872 | tf_op jit(solution)/shard_map/ppermute | solution.py:17
  80.2 23.3 %collective-permute-start.1 = (bf16[4,2,1,64,512]{4,3,2,1,0:T(8,128)(2,1)S(1)}, bf16[4,2,1,64,512]{4,3,2,1,0:T(8,128)(2,1)S(1)}, u32[]{:S(2)}, u32[]{:S(2)}) collective-permute-start(bf16[4,2,1,64,512]{4,3,2,1,0:T(8,128)(2,1)S(1)} %get-tuple-element.21), channel_id=1, source_target_pairs={{16,0},{32,16},{48,32},{64,48},{80,64},{96,80},{112,96},{17,1},{33... | collective-permute-start | bytes 1572872 | tf_op jit(solution)/shard_map/ppermute | solution.py:20
  123.7 8.5 %copy-start.20 = (bf16[2,4,64,512]{3,2,1,0:T(8,128)(2,1)S(1)}, bf16[2,4,64,512]{3,2,1,0:T(8,128)(2,1)}, u32[]{:S(2)}) copy-start(bf16[2,4,64,512]{3,2,1,0:T(8,128)(2,1)} %get-tuple-element.137) | copy-start | bytes 1572868
  123.7 8.5 %copy-start.29 = (f32[512,128]{1,0:T(8,128)S(1)}, f32[512,128]{1,0:T(8,128)}, u32[]{:S(2)}) copy-start(f32[512,128]{1,0:T(8,128)} %fusion.111) | copy-start | bytes 786436
  125.0 7.5 %copy-start.18 = (bf16[2,4,64,512]{3,2,1,0:T(8,128)(2,1)S(1)}, bf16[2,4,64,512]{3,2,1,0:T(8,128)(2,1)}, u32[]{:S(2)}) copy-start(bf16[2,4,64,512]{3,2,1,0:T(8,128)(2,1)} %get-tuple-element.143) | copy-start | bytes 1572868
  126.3 16.4 %collective-permute-start.4 = (bf16[2,1,64,32]{2,1,0,3:T(2,128)(2,1)S(1)}, bf16[2,1,64,32]{2,1,0,3:T(2,128)(2,1)S(1)}, u32[]{:S(2)}, u32[]{:S(2)}) collective-permute-start(bf16[2,1,64,32]{2,1,0,3:T(2,128)(2,1)S(1)} %get-tuple-element.121), channel_id=1, source_target_pairs={{0,16},{16,32},{32,48},{48,64},{64,80},{80,96},{96,112},{1,17},{17... | collective-permute-start | bytes 24584 | tf_op jit(solution)/shard_map/ppermute | solution.py:17
  130.1 12.7 %collective-permute-start.5 = (bf16[2,1,64,32]{2,1,0,3:T(2,128)(2,1)S(1)}, bf16[2,1,64,32]{2,1,0,3:T(2,128)(2,1)S(1)}, u32[]{:S(2)}, u32[]{:S(2)}) collective-permute-start(bf16[2,1,64,32]{2,1,0,3:T(2,128)(2,1)S(1)} %get-tuple-element.122), channel_id=1, source_target_pairs={{16,0},{32,16},{48,32},{64,48},{80,64},{96,80},{112,96},{17,1},{33... | collective-permute-start | bytes 24584 | tf_op jit(solution)/shard_map/ppermute | solution.py:20
  178.9 6.9 %copy-start.3 = (bf16[2,4,64,512]{3,2,1,0:T(8,128)(2,1)S(1)}, bf16[2,4,64,512]{3,2,1,0:T(8,128)(2,1)}, u32[]{:S(2)}) copy-start(bf16[2,4,64,512]{3,2,1,0:T(8,128)(2,1)} %get-tuple-element.45) | copy-start | bytes 1572868
  180.1 6.7 %collective-permute-start.6 = (bf16[2,1,64,32]{2,1,0,3:T(2,128)(2,1)S(1)}, bf16[2,1,64,32]{2,1,0,3:T(2,128)(2,1)S(1)}, u32[]{:S(2)}, u32[]{:S(2)}) collective-permute-start(bf16[2,1,64,32]{2,1,0,3:T(2,128)(2,1)S(1)} %get-tuple-element.119), channel_id=1, source_target_pairs={{0,16},{16,32},{32,48},{48,64},{64,80},{80,96},{96,112},{1,17},{17... | collective-permute-start | bytes 24584 | tf_op jit(solution)/shard_map/ppermute | solution.py:17
  183.9 5.6 %collective-permute-start.7 = (bf16[2,1,64,32]{2,1,0,3:T(2,128)(2,1)S(1)}, bf16[2,1,64,32]{2,1,0,3:T(2,128)(2,1)S(1)}, u32[]{:S(2)}, u32[]{:S(2)}) collective-permute-start(bf16[2,1,64,32]{2,1,0,3:T(2,128)(2,1)S(1)} %get-tuple-element.120), channel_id=1, source_target_pairs={{16,0},{32,16},{48,32},{64,48},{80,64},{96,80},{112,96},{17,1},{33... | collective-permute-start | bytes 24584 | tf_op jit(solution)/shard_map/ppermute | solution.py:20
  224.9 6.1 %copy-start.2 = (bf16[2,4,64,512]{3,2,1,0:T(8,128)(2,1)S(1)}, bf16[2,4,64,512]{3,2,1,0:T(8,128)(2,1)}, u32[]{:S(2)}) copy-start(bf16[2,4,64,512]{3,2,1,0:T(8,128)(2,1)} %get-tuple-element.139) | copy-start | bytes 1572868
  224.9 6.1 %copy-start.30 = (f32[512,128]{1,0:T(8,128)S(1)}, f32[512,128]{1,0:T(8,128)}, u32[]{:S(2)}) copy-start(f32[512,128]{1,0:T(8,128)} %convolution_add_fusion.58) | copy-start | bytes 786436
  225.7 5.6 %collective-permute-start.8 = (bf16[2,1,64,32]{2,1,0,3:T(2,128)(2,1)S(1)}, bf16[2,1,64,32]{2,1,0,3:T(2,128)(2,1)S(1)}, u32[]{:S(2)}, u32[]{:S(2)}) collective-permute-start(bf16[2,1,64,32]{2,1,0,3:T(2,128)(2,1)S(1)} %get-tuple-element.117), channel_id=1, source_target_pairs={{0,16},{16,32},{32,48},{48,64},{64,80},{80,96},{96,112},{1,17},{17... | collective-permute-start | bytes 24584 | tf_op jit(solution)/shard_map/ppermute | solution.py:17
  227.7 5.6 %collective-permute-start.9 = (bf16[2,1,64,32]{2,1,0,3:T(2,128)(2,1)S(1)}, bf16[2,1,64,32]{2,1,0,3:T(2,128)(2,1)S(1)}, u32[]{:S(2)}, u32[]{:S(2)}) collective-permute-start(bf16[2,1,64,32]{2,1,0,3:T(2,128)(2,1)S(1)} %get-tuple-element.118), channel_id=1, source_target_pairs={{16,0},{32,16},{48,32},{64,48},{80,64},{96,80},{112,96},{17,1},{33... | collective-permute-start | bytes 24584 | tf_op jit(solution)/shard_map/ppermute | solution.py:20
  270.1 11.7 %all-to-all-start = ((bf16[16,2,512]{2,1,0:T(2,128)(2,1)}), bf16[16,2,512]{2,1,0:T(2,128)(2,1)S(1)}, u32[]{:S(2)}, u32[]{:S(2)}) async-start(bf16[16,2,512]{2,1,0:T(2,128)(2,1)} %reshape.550), calls=%async_computation | async-start | bytes 65536 | tf_op jit(solution)/shard_map/all_to_all | solution.py:85
  282.2 5.3 %collective-permute-start.10 = (bf16[2,2,4,512]{3,2,1,0:T(4,128)(2,1)S(1)}, bf16[2,2,4,512]{3,2,1,0:T(4,128)(2,1)S(1)}, u32[]{:S(2)}, u32[]{:S(2)}) collective-permute-start(bf16[2,2,4,512]{3,2,1,0:T(4,128)(2,1)S(1)} %get-tuple-element.126), channel_id=1, source_target_pairs={{0,16},{16,32},{32,48},{48,64},{64,80},{80,96},{96,112},{1,17},{17... | collective-permute-start | bytes 49160 | tf_op jit(solution)/shard_map/ppermute | solution.py:17
  284.8 5.4 %collective-permute-start.11 = (bf16[2,2,4,512]{3,2,1,0:T(4,128)(2,1)S(1)}, bf16[2,2,4,512]{3,2,1,0:T(4,128)(2,1)S(1)}, u32[]{:S(2)}, u32[]{:S(2)}) collective-permute-start(bf16[2,2,4,512]{3,2,1,0:T(4,128)(2,1)S(1)} %get-tuple-element.125), channel_id=1, source_target_pairs={{16,0},{32,16},{48,32},{64,48},{80,64},{96,80},{112,96},{17,1},{33... | collective-permute-start | bytes 49160 | tf_op jit(solution)/shard_map/ppermute | solution.py:20
  290.2 6.6 %collective-permute-start.12 = (bf16[2,8,2,512]{3,2,1,0:T(2,128)(2,1)S(1)}, bf16[2,8,2,512]{3,2,1,0:T(2,128)(2,1)S(1)}, u32[]{:S(2)}, u32[]{:S(2)}) collective-permute-start(bf16[2,8,2,512]{3,2,1,0:T(2,128)(2,1)S(1)} %get-tuple-element.115), channel_id=1, source_target_pairs={{0,1},{1,2},{2,3},{3,4},{4,5},{5,6},{6,7},{7,8},{8,9},{9,10},{10,1... | collective-permute-start | bytes 98312 | tf_op jit(solution)/shard_map/ppermute | solution.py:17
  294.1 5.2 %collective-permute-start.13 = (bf16[2,8,2,512]{3,2,1,0:T(2,128)(2,1)S(1)}, bf16[2,8,2,512]{3,2,1,0:T(2,128)(2,1)S(1)}, u32[]{:S(2)}, u32[]{:S(2)}) collective-permute-start(bf16[2,8,2,512]{3,2,1,0:T(2,128)(2,1)S(1)} %get-tuple-element.116), channel_id=1, source_target_pairs={{1,0},{2,1},{3,2},{4,3},{5,4},{6,5},{7,6},{8,7},{9,8},{10,9},{11,1... | collective-permute-start | bytes 98312 | tf_op jit(solution)/shard_map/ppermute | solution.py:20
  (29 other events, 44.0 us)
Sparse Core Ops, SparseCore 0:
  10.5 59.8 all-gather.1
where the time goes:
time: 336 us; the launch traced here: 331 us
  blocking collectives  113 us (34%)
  waiting for transfers between devices  55.2 us (16%)
  matrix products  48.6 us (14%)
  local copies, waits for them, and re-layouts  48 us (14%)
  starting transfers between devices  43.7 us (13%)
  between operations  15.4 us (5%)
  other arithmetic  6.69 us (2%)
    all_gather x4, blocking collectives, per_device(): rimmed = lax.all_gather(edged, 'hid', axis=3, tiled=True)  113 us
    dot_general x90, matrix products, conv_taps(): jnp.dot(window.reshape(-1, channel_count), weight[tap_row, tap_col], pref...  48.6 us
    ppermute x7, waiting for transfers between devices, extended_2(): lax.ppermute(lax.slice_in_dim(block, 0, width, axis=dim), axis, backward)  25 us
    ppermute x7, starting transfers between devices, extended_2(): lax.ppermute(lax.slice_in_dim(block, block.shape[dim] - width, None, axis...  23.2 us
    ppermute x7, starting transfers between devices, extended_2(): lax.ppermute(lax.slice_in_dim(block, 0, width, axis=dim), axis, backward)  16.1 us
    all_gather x1, waiting for transfers between devices, per_device(): all_frames = lax.all_gather(frames, 'hid', axis=4, tiled=True)  14.9 us
    slice x8, local copies, waits for them, and re-layouts, conv_taps(): padded[:, tap_row:tap_row + row_count, tap_col:tap_col + col_count, :]  13.2 us
    all_gather x4, local copies, waits for them, and re-layouts, per_device(): rimmed = lax.all_gather(edged, 'hid', axis=3, tiled=True)  12.6 us
  transfers between devices with their start and end apart: 16, of which 9 were waited for; matrix products, arithmetic and copies ran while one was open for 5% of the time, Pallas kernels for 0%

commit v1 on v0

v1 whole, which is shorter than its diff:
```python
import jax
import jax.numpy as jnp
from jax import lax
from jax.experimental import pallas as pl
from jax.experimental.pallas import tpu as pltpu
from jax.sharding import PartitionSpec as P

STEPS = 4
MESH = pl.DeviceIdType.MESH
F32 = jnp.float32
BF16 = jnp.bfloat16


def swap_halves(tile):
    return jnp.concatenate([tile[..., 64:], tile[..., :64]], axis=-1)


def kernel(
    frames, hidden, cell_in, gate_bias, bias1, bias2, w_in, w_hid, w_first, w_second,
    decoded, cell_out,
    packed, packed_cell, own, edge_top, edge_bot, image, halo_top, halo_bot,
    far_top_out, far_bot_out, far_top, far_bot,
    wi, wh, w1, w2, bias_col, cell, gin, dec_out, dec_in, cell_back,
    w_sem, wx_send, wx_recv, s1_send, s1_recv, c1_send, c1_recv, local_sem,
    x_send, x_recv, ht_send, ht_recv, hb_send, hb_recv, fin_send, fin_recv, c2_send, c2_recv, d_send, d_recv,
):
    patch = lax.axis_index("patch")
    hid = lax.axis_index("hid")
    core = lax.rem(hid, 2)
    grp = hid // 2
    x_hi = grp // 4
    y = patch // 2
    x_lo = lax.rem(patch, 2)
    flip = lax.rem(x_hi + y, 2)
    block = y * 2 + lax.rem(x_lo + flip, 2)

    def holder(blk, g, c):
        by = blk // 2
        lo = lax.rem(lax.rem(blk, 2) + g // 4 + by, 2)
        return (by * 2 + lo, g * 2 + c)

    def trade(c):
        return (y * 2 + lax.rem(x_lo + flip, 2), grp * 2 + c)

    has_up = block > 0
    has_down = block < 7
    sibling = (patch, grp * 2 + 1 - core)

    def peer(d):
        g = lax.rem(grp // 4 + d // 4, 2) * 4 + lax.rem(lax.rem(grp, 4) + lax.rem(d, 4), 4)
        return g

    barrier = pltpu.get_barrier_semaphore()

    def greet(device):
        pl.semaphore_signal(barrier, inc=1, device_id=device, device_id_type=MESH)

    greet(sibling)

    @pl.when(flip == 1)
    def _():
        greet(trade(0))
        greet(trade(1))

    @pl.loop(1, 8)
    def _(d):
        greet(holder(block, peer(d), core))

    @pl.loop(0, 8)
    def _(g):
        @pl.when(has_up)
        def _():
            greet(holder(block - 1, g, core))

        @pl.when(has_down)
        def _():
            greet(holder(block + 1, g, core))

    weight_copies = []
    for k, (src, dst) in enumerate(((w_in, wi), (w_hid, wh))):
        copy = pltpu.make_async_copy(src, dst.at[:, :, core], w_sem.at[k])
        copy.start()
        weight_copies.append(copy)
    for k, (src, dst) in enumerate(((w_first, w1), (w_second, w2))):
        copy = pltpu.make_async_copy(src, dst, w_sem.at[2 + k])
        copy.start()
        weight_copies.append(copy)

    for b in range(2):
        for t in range(STEPS):
            packed[b, t] = jnp.concatenate([frames[t, b, r] for r in (0, 2, 1, 3)], axis=-1)
        packed[b, STEPS] = jnp.concatenate([hidden[b, r] for r in (0, 2, 1, 3)], axis=-1)
        packed_cell[b] = jnp.concatenate([cell_in[b, r] for r in (0, 2, 1, 3)], axis=-1)
    eye = lax.broadcasted_iota(jnp.int32, (32, 32), 0) == lax.broadcasted_iota(jnp.int32, (32, 32), 1)
    for k in range(4):
        column = jnp.sum(jnp.where(eye, gate_bias[k : k + 1, :], 0.0), axis=1, keepdims=True)
        bias_col[core, k * 32 : (k + 1) * 32, :] = jnp.broadcast_to(column, (32, 128))

    @pl.when(block == 0)
    def _():
        halo_top[...] = jnp.zeros_like(halo_top)
        far_top[...] = jnp.zeros_like(far_top)

    @pl.when(block == 7)
    def _():
        halo_bot[...] = jnp.zeros_like(halo_bot)
        far_bot[...] = jnp.zeros_like(far_bot)

    greeted = 1 + 2 * flip + 7 + jnp.where(has_up, 8, 0) + jnp.where(has_down, 8, 0)
    pl.semaphore_wait(barrier, greeted)

    my_rows = pl.ds(pl.multiple_of(core * 32, 32), 32)

    def trade_copies(c, b, rows):
        return (
            pltpu.make_async_remote_copy(
                src_ref=packed.at[b], dst_ref=own.at[0 : STEPS + 1, rows, :],
                send_sem=s1_send.at[b], recv_sem=s1_recv.at[c],
                device_id=trade(b), device_id_type=MESH,
            ),
            pltpu.make_async_remote_copy(
                src_ref=packed_cell.at[b], dst_ref=cell.at[c],
                send_sem=c1_send.at[b], recv_sem=c1_recv.at[c],
                device_id=trade(b), device_id_type=MESH,
            ),
        )

    for b in range(2):
        stays = (flip == 0) & (core == b)

        @pl.when(jnp.logical_not(stays))
        def _(b=b):
            for copy in trade_copies(core, b, my_rows):
                copy.start()

        @pl.when(stays)
        def _(b=b):
            one = pltpu.make_async_copy(packed.at[b], own.at[0 : STEPS + 1, my_rows, :], local_sem.at[0])
            two = pltpu.make_async_copy(packed_cell.at[b], cell.at[core], local_sem.at[1])
            one.start()
            two.start()
            one.wait()
            two.wait()

    def weight_trade(k, src, dst):
        return pltpu.make_async_remote_copy(
            src_ref=src, dst_ref=dst, send_sem=wx_send.at[k], recv_sem=wx_recv.at[k],
            device_id=sibling, device_id_type=MESH,
        )

    trades = [
        weight_trade(0, w_in, wi.at[:, :, core]),
        weight_trade(1, w_hid, wh.at[:, :, core]),
        weight_trade(2, bias_col.at[core], bias_col.at[core]),
    ]
    for copy in trades:
        copy.start()

    for c in range(2):
        stays = (flip == 0) & (core == c)

        @pl.when(jnp.logical_not(stays))
        def _(c=c):
            for copy in trade_copies(c, 0, pl.ds(c * 32, 32)):
                copy.wait_recv()

    half = lax.broadcasted_iota(jnp.int32, (32, 128), 1) < 64
    my_tile = pl.ds(pl.multiple_of(grp * 64, 64), 64)
    my_edge = pl.ds(pl.multiple_of(grp * 32, 32), 32)

    def pack_edges(slot):
        a = own[slot, :, 0:128]
        b = own[slot, :, 128:256]
        edge_top[slot] = jnp.where(half, a[:32], swap_halves(a[32:]))
        edge_bot[slot] = jnp.where(half, swap_halves(b[:32]), b[32:])

    def tile_copy(slot, d):
        return pltpu.make_async_remote_copy(
            src_ref=own.at[slot], dst_ref=image.at[slot, my_tile, 128:384],
            send_sem=x_send.at[slot], recv_sem=x_recv.at[slot],
            device_id=holder(block, peer(d), core), device_id_type=MESH,
        )

    def up_copy(slot, g):
        return pltpu.make_async_remote_copy(
            src_ref=edge_top.at[slot], dst_ref=halo_bot.at[slot, my_edge, :],
            send_sem=ht_send.at[slot], recv_sem=hb_recv.at[slot],
            device_id=holder(block - 1, g, core), device_id_type=MESH,
        )

    def down_copy(slot, g):
        return pltpu.make_async_remote_copy(
            src_ref=edge_bot.at[slot], dst_ref=halo_top.at[slot, my_edge, :],
            send_sem=hb_send.at[slot], recv_sem=ht_recv.at[slot],
            device_id=holder(block + 1, g, core), device_id_type=MESH,
        )

    def send_tiles(slot):
        image[slot, my_tile, 128:384] = own[slot]

        @pl.loop(1, 8)
        def _(k):
            tile_copy(slot, 8 - k).start()

    def broadcast(slot):
        pack_edges(slot)

        @pl.loop(0, 8)
        def _(g):
            @pl.when(has_up)
            def _():
                up_copy(slot, g).start()

            @pl.when(has_down)
            def _():
                down_copy(slot, g).start()

        send_tiles(slot)

    def wait_bytes(ref, sem):
        pltpu.make_async_copy(ref, ref, sem).wait()

    def wait_tiles(slot):
        wait_bytes(image.at[slot, 0:448, 128:384], x_recv.at[slot])

    def wait_sent(slot):
        wait_bytes(image.at[slot, 0:448, 128:384], x_send.at[slot])

        @pl.when(has_up)
        def _():
            wait_bytes(halo_top.at[slot], ht_send.at[slot])

        @pl.when(has_down)
        def _():
            wait_bytes(halo_bot.at[slot], hb_send.at[slot])

    def wait_image(slot):
        wait_tiles(slot)

        @pl.when(has_up)
        def _():
            wait_bytes(halo_top.at[slot], ht_recv.at[slot])

        @pl.when(has_down)
        def _():
            wait_bytes(halo_bot.at[slot], hb_recv.at[slot])

        for g in range(8):
            a0 = image[slot, g * 64 : g * 64 + 32, 128:256]
            a1 = image[slot, g * 64 + 32 : g * 64 + 64, 128:256]
            b0 = image[slot, g * 64 : g * 64 + 32, 256:384]
            b1 = image[slot, g * 64 + 32 : g * 64 + 64, 256:384]
            top = halo_top[slot, g * 32 : g * 32 + 32, :]
            bot = halo_bot[slot, g * 32 : g * 32 + 32, :]
            image[slot, g * 64 : g * 64 + 32, 0:128] = jnp.where(half, top, swap_halves(b0))
            image[slot, g * 64 + 32 : g * 64 + 64, 0:128] = swap_halves(jnp.where(half, b1, top))
            image[slot, g * 64 : g * 64 + 32, 384:512] = swap_halves(jnp.where(half, bot, a0))
            image[slot, g * 64 + 32 : g * 64 + 64, 384:512] = jnp.where(half, swap_halves(a1), bot)

    place = lax.rem(lax.broadcasted_iota(jnp.int32, (256, 128), 1), 64)

    def conv(slot, weight, write):
        parts = []
        for q in range(3):
            total = None
            for p in range(3):
                lhs = weight[p, q].reshape(256, 512)
                term = jnp.dot(lhs, image[slot, :, p * 128 : p * 128 + 256], preferred_element_type=F32)
                total = term if total is None else total + term
            parts.append(total)
        for tile in range(2):
            lanes = slice(tile * 128, (tile + 1) * 128)
            left = jnp.where(place == 0, 0.0, pltpu.roll(parts[0][:, lanes], 1, 1))
            right = jnp.where(place == 63, 0.0, pltpu.roll(parts[2][:, lanes], 127, 1))
            write(lanes, parts[1][:, lanes] + left + right)

    broadcast(0)
    broadcast(STEPS)
    weight_copies[0].wait()
    weight_copies[1].wait()
    for k, copy in enumerate(trades):
        copy.wait_recv()

    def write_gin(lanes, value):
        for c in range(2):
            rows = slice(c * 128, (c + 1) * 128)
            gin[rows, lanes] = value[rows] + bias_col[c]

    def update(next_slot):
        def write(lanes, value):
            gates = value + gin[:, lanes]
            for c in range(2):
                z = [gates[c * 128 + k * 32 : c * 128 + (k + 1) * 32] for k in range(4)]
                new = jax.nn.sigmoid(z[1] + 1.0) * cell[c, :, lanes] + jax.nn.sigmoid(z[0]) * jnp.tanh(z[2])
                cell[c, :, lanes] = new
                own[next_slot, c * 32 : (c + 1) * 32, lanes] = (jax.nn.sigmoid(z[3]) * jnp.tanh(new)).astype(BF16)

        return write

    def step(t, carry):
        slot = STEPS + lax.rem(t, 2)
        following = STEPS + lax.rem(t + 1, 2)

        @pl.when(t < STEPS - 1)
        def _():
            broadcast(t + 1)

        wait_image(t)
        conv(t, wi, write_gin)
        wait_image(slot)

        @pl.when(t > 0)
        def _():
            wait_sent(following)

        conv(slot, wh, update(following))

        @pl.when(t < STEPS - 1)
        def _():
            broadcast(following)

        return carry

    lax.fori_loop(0, STEPS, step, 0)

    last = STEPS + STEPS % 2
    wide = lax.broadcasted_iota(jnp.int32, (64, 128), 1) < 64
    row_a = own[last, :, 0:128]
    row_b = own[last, :, 128:256]
    far_top_out[...] = jnp.where(wide, row_a, swap_halves(row_b))
    far_bot_out[...] = jnp.where(wide, swap_halves(row_a), row_b)

    def far_up_copy(g):
        return pltpu.make_async_remote_copy(
            src_ref=far_top_out, dst_ref=far_bot.at[my_tile, :],
            send_sem=fin_send.at[0], recv_sem=fin_recv.at[0],
            device_id=holder(block - 1, g, core), device_id_type=MESH,
        )

    def far_down_copy(g):
        return pltpu.make_async_remote_copy(
            src_ref=far_bot_out, dst_ref=far_top.at[my_tile, :],
            send_sem=fin_send.at[1], recv_sem=fin_recv.at[1],
            device_id=holder(block + 1, g, core), device_id_type=MESH,
        )

    @pl.loop(0, 8)
    def _(g):
        @pl.when(has_up)
        def _():
            far_up_copy(g).start()

        @pl.when(has_down)
        def _():
            far_down_copy(g).start()

    send_tiles(last)

    def cell_copy(c, b):
        return pltpu.make_async_remote_copy(
            src_ref=cell.at[c], dst_ref=cell_back.at[b],
            send_sem=c2_send.at[c], recv_sem=c2_recv.at[b],
            device_id=trade(c), device_id_type=MESH,
        )

    for c in range(2):
        stays = (flip == 0) & (core == c)

        @pl.when(jnp.logical_not(stays))
        def _(c=c):
            cell_copy(c, core).start()

        @pl.when(stays)
        def _(c=c):
            copy = pltpu.make_async_copy(cell.at[c], cell_back.at[core], local_sem.at[1])
            copy.start()
            copy.wait()

    weight_copies[2].wait()
    weight_copies[3].wait()
    wait_tiles(last)

    @pl.when(has_down)
    def _():
        wait_bytes(far_bot, fin_recv.at[0])

    @pl.when(has_up)
    def _():
        wait_bytes(far_top, fin_recv.at[1])

    sel_row = lax.broadcasted_iota(jnp.int32, (32, 128), 0)
    sel_lane = lax.broadcasted_iota(jnp.int32, (32, 128), 1)
    want = lax.rem(sel_row, 16) + grp * 8 - 2
    chosen = (want >= 0) & (want < 64) & (sel_lane == want + 64 * (sel_row // 16))
    pick = jnp.where(chosen, 1.0, 0.0).astype(BF16)

    def window(tile):
        return lax.dot_general(pick, tile, (((1,), (1,)), ((), ())), preferred_element_type=F32).astype(BF16)

    above = window(far_top[...])
    tile_a = window(image[last, :, 128:256])
    tile_b = window(image[last, :, 256:384])
    below = window(far_bot[...])
    pixels = jnp.concatenate([above, tile_a[:16], tile_b[:16], tile_a[16:], tile_b[16:], below], axis=0)

    def decode(source, rows, weight):
        parts = []
        for q in range(3):
            total = None
            for p in range(3):
                term = jnp.dot(source[p * 16 : p * 16 + rows * 16], weight[p, q], preferred_element_type=F32)
                total = term if total is None else total + term
            parts.append(total)
        return parts[1] + pltpu.roll(parts[0], 1, 0) + pltpu.roll(parts[2], rows * 16 - 1, 0)

    first = decode(pixels, 6, w1) + bias1[...]
    first = first / (1.0 + jnp.exp(-first))
    pixel = lax.broadcasted_iota(jnp.int32, (96, 512), 0)
    image_row = block * 4 - 1 + pixel // 16
    image_col = grp * 8 - 2 + lax.rem(pixel, 16)
    inside = (image_row >= 0) & (image_row < 32) & (image_col >= 0) & (image_col < 64)
    middle = jnp.where(inside, first, 0.0).astype(BF16)
    second = decode(middle, 4, w2) + bias2[...]
    shifted = second.reshape(4, 16, 512)
    for c in range(2):
        dec_out[c] = shifted[:, 2 + 4 * c : 6 + 4 * c, :].astype(BF16)

    def dec_copy(c, b):
        return pltpu.make_async_remote_copy(
            src_ref=dec_out.at[c], dst_ref=dec_in.at[b],
            send_sem=d_send.at[c], recv_sem=d_recv.at[b],
            device_id=trade(c), device_id_type=MESH,
        )

    for c in range(2):
        stays = (flip == 0) & (core == c)

        @pl.when(jnp.logical_not(stays))
        def _(c=c):
            dec_copy(c, core).start()

        @pl.when(stays)
        def _(c=c):
            dec_in[core] = dec_out[c]

    for b in range(2):
        stays = (flip == 0) & (core == b)

        @pl.when(jnp.logical_not(stays))
        def _(b=b):
            cell_copy(0, b).wait_recv()

        for r in range(4):
            start = (r % 2) * 128 + (r // 2) * 64
            cell_out[b, r] = cell_back[b, :, start : start + 64]

    for slot in range(STEPS):
        wait_sent(slot)
    wait_sent(STEPS + 1)
    wait_bytes(image.at[last, 0:448, 128:384], x_send.at[last])

    @pl.when(has_up)
    def _():
        wait_bytes(far_top, fin_send.at[0])

    @pl.when(has_down)
    def _():
        wait_bytes(far_bot, fin_send.at[1])

    for copy in trades:
        copy.wait_send()

    for b in range(2):
        stays = (flip == 0) & (core == b)

        @pl.when(jnp.logical_not(stays))
        def _(b=b):
            for copy in trade_copies(core, b, my_rows):
                copy.wait_send()
            cell_copy(b, core).wait_send()
            dec_copy(0, b).wait_recv()
            dec_copy(b, core).wait_send()

        decoded[b] = dec_in[b]


def per_device(
    frames, hidden_start, cell_start, input_weight, hidden_weight, gate_bias,
    first_weight, first_bias, second_weight, second_bias,
):
    vmem = pl.BlockSpec(memory_space=pltpu.VMEM)
    anywhere = pl.BlockSpec(memory_space=pl.ANY)
    dma = pltpu.SemaphoreType.DMA
    slots = STEPS + 2

    def gate_rows(weight):
        return weight.transpose(0, 1, 3, 4, 2).reshape(3, 3, 128, 512)

    decoded, cell = pl.pallas_call(
        kernel,
        name="convlstm",
        out_shape=(
            jax.ShapeDtypeStruct((2, 4, 4, 512), BF16),
            jax.ShapeDtypeStruct((2, 4, 32, 64), F32),
        ),
        in_specs=[vmem] * 6 + [anywhere] * 4,
        out_specs=(vmem, vmem),
        scratch_shapes=[
            pltpu.VMEM((2, STEPS + 1, 32, 256), BF16),
            pltpu.VMEM((2, 32, 256), F32),
            pltpu.VMEM((slots, 64, 256), BF16),
            pltpu.VMEM((slots, 32, 128), BF16),
            pltpu.VMEM((slots, 32, 128), BF16),
            pltpu.VMEM((slots, 512, 512), BF16),
            pltpu.VMEM((slots, 256, 128), BF16),
            pltpu.VMEM((slots, 256, 128), BF16),
            pltpu.VMEM((64, 128), BF16),
            pltpu.VMEM((64, 128), BF16),
            pltpu.VMEM((512, 128), BF16),
            pltpu.VMEM((512, 128), BF16),
            pltpu.VMEM((3, 3, 2, 128, 512), BF16),
            pltpu.VMEM((3, 3, 2, 128, 512), BF16),
            pltpu.VMEM((3, 3, 512, 512), BF16),
            pltpu.VMEM((3, 3, 512, 512), BF16),
            pltpu.VMEM((2, 128, 128), F32),
            pltpu.VMEM((2, 32, 256), F32),
            pltpu.VMEM((256, 256), F32),
            pltpu.VMEM((2, 4, 4, 512), BF16),
            pltpu.VMEM((2, 4, 4, 512), BF16),
            pltpu.VMEM((2, 32, 256), F32),
            dma((4,)), dma((3,)), dma((3,)), dma((2,)), dma((2,)), dma((2,)), dma((2,)), dma((2,)),
            dma((slots,)), dma((slots,)), dma((slots,)), dma((slots,)), dma((slots,)), dma((slots,)),
            dma((2,)), dma((2,)), dma((2,)), dma((2,)), dma((2,)), dma((2,)),
        ],
        compiler_params=pltpu.CompilerParams(
            collective_id=0, has_side_effects=True, vmem_limit_bytes=50 << 20
        ),
    )(
        frames.transpose(0, 1, 2, 4, 3),
        hidden_start.transpose(0, 1, 3, 2),
        cell_start.transpose(0, 1, 3, 2),
        gate_bias,
        first_bias.reshape(1, -1),
        second_bias.reshape(1, -1),
        gate_rows(input_weight),
        gate_rows(hidden_weight),
        first_weight,
        second_weight,
    )
    return decoded, cell.transpose(0, 1, 3, 2)


def solution(mesh):
    return jax.shard_map(
        per_device,
        mesh=mesh,
        in_specs=(
            P(None, None, "patch", None, "hid"),
            P(None, "patch", None, "hid"),
            P(None, "patch", None, "hid"),
            P(None, None, None, None, "hid"),
            P(None, None, None, None, "hid"),
            P(None, "hid"),
            P(),
            P(),
            P(),
            P(),
        ),
        out_specs=(P(None, "patch", "hid", None), P(None, "patch", None, "hid")),
        check_vma=False,
    )
```

time: 336 us -> 75.5 us (0.22); the launches traced: 331 us -> 75.1 us
  blocking collectives: 113 us -> 0 us
  Pallas kernels: 0 us -> 65.9 us
  waiting for transfers between devices: 55.2 us -> 0 us
  matrix products: 48.6 us -> 0 us
  starting transfers between devices: 43.7 us -> 0 us
  local copies, waits for them, and re-layouts: 48 us -> 8.54 us
  between operations: 15.4 us -> 0.66 us
  other arithmetic: 6.69 us -> 0 us
    all_gather x4 -> x0, blocking collectives: 113 us -> none  [per_device(): rimmed = lax.all_gather(edged, 'hid', axis=3, tiled=True)]
    pallas_call x0 -> x1, Pallas kernels: none -> 65.9 us  [per_device(): pl.pallas_call(kernel, name='convlstm', out_shape=(jax.ShapeDtypeStruct((...]
    dot_general x90 -> x0, matrix products: 48.6 us -> none  [conv_taps(): jnp.dot(window.reshape(-1, channel_count), weight[tap_row, tap_col], pref...]
    ppermute x14 -> x0, starting transfers between devices: 39.2 us -> none  [the longest x7 23.2 us: extended_2(): lax.ppermute(lax.slice_in_dim(block, block.shape[dim] - width, None, axis...]
    ppermute x14 -> x0, waiting for transfers between devices: 32.9 us -> none  [the longest x7 25 us: extended_2(): lax.ppermute(lax.slice_in_dim(block, 0, width, axis=dim), axis, backward)]
    all_gather x5 -> x0, local copies, waits for them, and re-layouts: 18.1 us -> none  [the longest x4 12.6 us: per_device(): rimmed = lax.all_gather(edged, 'hid', axis=3, tiled=True)]
    all_gather x1 -> x0, waiting for transfers between devices: 14.9 us -> none  [per_device(): all_frames = lax.all_gather(frames, 'hid', axis=4, tiled=True)]
    slice x15 -> x0, local copies, waits for them, and re-layouts: 13.5 us -> none  [the longest x8 13.2 us: conv_taps(): padded[:, tap_row:tap_row + row_count, tap_col:tap_col + col_count, :]]
  transfers between devices with their start and end apart: 16 -> 0, of which waited for: 9 -> 0; matrix products, arithmetic and copies ran while one was open for 5% -> 0% of each run, Pallas kernels for 0% -> 0%
where the time goes in v1:
time: 75.5 us; the launch traced here: 75.1 us
  Pallas kernels  65.9 us (87%)
  local copies, waits for them, and re-layouts  8.54 us (11%)
    pallas_call x1, Pallas kernels, per_device(): pl.pallas_call(kernel, name='convlstm', out_shape=(jax.ShapeDtypeStruct((...  65.9 us
    unnamed x18, local copies, waits for them, and re-layouts  8.54 us

profile of v1, /device:TPU:11, one launch (start us, length us, event | category | flops | bytes accessed | tf_op | source)
XLA Modules:
  0.0 75.1 jit_solution(6085167876173991437)
XLA Ops:
  0.6 0.0 copy-start
  0.6 1.3 %copy-done = bf16[3,3,512,4,32]{2,4,3,1,0:T(8,128)(2,1)S(1)} copy-done((bf16[3,3,512,4,32]{2,4,3,1,0:T(8,128)(2,1)S(1)}, bf16[3,3,512,4,32]{2,4,3,1,0:T(8,128)(2,1)}, u32[]{:S(2)}) %copy-start) | copy-done | bytes 1179672
  1.9 0.0 copy-start.1
  1.9 1.3 %copy-done.1 = bf16[3,3,512,4,32]{2,4,3,1,0:T(8,128)(2,1)S(1)} copy-done((bf16[3,3,512,4,32]{2,4,3,1,0:T(8,128)(2,1)S(1)}, bf16[3,3,512,4,32]{2,4,3,1,0:T(8,128)(2,1)}, u32[]{:S(2)}) %copy-start.1) | copy-done | bytes 1179672
  3.2 0.0 copy-start.2
  3.2 0.9 %copy-done.2 = bf16[4,2,4,64,32]{3,4,2,1,0:T(8,128)(2,1)S(1)} copy-done((bf16[4,2,4,64,32]{3,4,2,1,0:T(8,128)(2,1)S(1)}, bf16[4,2,4,64,32]{3,4,2,1,0:T(8,128)(2,1)}, u32[]{:S(2)}) %copy-start.2) | copy-done | bytes 131096
  4.1 0.0 copy-start.3
  4.1 0.9 %copy-done.3 = f32[2,4,64,32]{2,3,1,0:T(8,128)S(1)} copy-done((f32[2,4,64,32]{2,3,1,0:T(8,128)S(1)}, f32[2,4,64,32]{2,3,1,0:T(8,128)}, u32[]{:S(2)}) %copy-start.3) | copy-done | bytes 65560
  5.0 0.0 copy-start.4
  5.0 0.8 %copy-done.4 = bf16[2,4,64,32]{2,3,1,0:T(8,128)(2,1)S(1)} copy-done((bf16[2,4,64,32]{2,3,1,0:T(8,128)(2,1)S(1)}, bf16[2,4,64,32]{2,3,1,0:T(8,128)(2,1)}, u32[]{:S(2)}) %copy-start.4) | copy-done | bytes 32792
  5.9 0.0 copy-start.5
  5.9 0.7 copy-done.5
  6.6 0.0 copy-start.6
  6.6 0.7 copy-done.6
  7.2 0.0 copy-start.7
  7.2 0.7 copy-done.7
  7.9 65.9 %convlstm.1 = (bf16[2,4,4,512]{3,2,1,0:T(4,128)(2,1)S(1)}, f32[2,4,32,64]{3,2,1,0:T(8,128)S(1)}) custom-call(bf16[4,2,4,32,64]{4,3,2,1,0:T(8,128)(2,1)S(1)} %bitcast.14, bf16[2,4,32,64]{3,2,1,0:T(8,128)(2,1)S(1)} %bitcast.17, f32[2,4,32,64]{3,2,1,0:T(8,128)S(1)} %bitcast.15, f32[4,32]{1,0:T(4,128)S(1)} %copy-done.5, f32[1,512]{1,0:T(1,128)S(1)} %bitcast.18, ...), custom_call_target="tpu_custom_call" | custom-call | tf_op jit(solution)/shard_map/convlstm/pallas_call | solution.py:499
  73.8 0.6 copy.14
  74.5 0.7 copy.15
Async XLA Ops:
  0.6 1.3 %copy-start = (bf16[3,3,512,4,32]{2,4,3,1,0:T(8,128)(2,1)S(1)}, bf16[3,3,512,4,32]{2,4,3,1,0:T(8,128)(2,1)}, u32[]{:S(2)}) copy-start(bf16[3,3,512,4,32]{2,4,3,1,0:T(8,128)(2,1)} %param.13) | copy-start | bytes 3538948
  1.9 1.3 %copy-start.1 = (bf16[3,3,512,4,32]{2,4,3,1,0:T(8,128)(2,1)S(1)}, bf16[3,3,512,4,32]{2,4,3,1,0:T(8,128)(2,1)}, u32[]{:S(2)}) copy-start(bf16[3,3,512,4,32]{2,4,3,1,0:T(8,128)(2,1)} %param.14) | copy-start | bytes 3538948
  3.2 0.9 %copy-start.2 = (bf16[4,2,4,64,32]{3,4,2,1,0:T(8,128)(2,1)S(1)}, bf16[4,2,4,64,32]{3,4,2,1,0:T(8,128)(2,1)}, u32[]{:S(2)}) copy-start(bf16[4,2,4,64,32]{3,4,2,1,0:T(8,128)(2,1)} %param.10) | copy-start | bytes 393220
  4.1 0.9 %copy-start.3 = (f32[2,4,64,32]{2,3,1,0:T(8,128)S(1)}, f32[2,4,64,32]{2,3,1,0:T(8,128)}, u32[]{:S(2)}) copy-start(f32[2,4,64,32]{2,3,1,0:T(8,128)} %param.12) | copy-start | bytes 196612
  5.0 0.8 %copy-start.4 = (bf16[2,4,64,32]{2,3,1,0:T(8,128)(2,1)S(1)}, bf16[2,4,64,32]{2,3,1,0:T(8,128)(2,1)}, u32[]{:S(2)}) copy-start(bf16[2,4,64,32]{2,3,1,0:T(8,128)(2,1)} %param.11) | copy-start | bytes 98308
  5.9 0.7 copy-start.5
  6.6 0.7 copy-start.6
  7.2 0.7 copy-start.7

commit v2 on v1

--- a/solution.py
+++ b/solution.py
@@ -6,6 +6,7 @@
 from jax.sharding import PartitionSpec as P
 
 STEPS = 4
+FAR_FIRST = (6, 5, 7, 2, 4, 1, 3)
 MESH = pl.DeviceIdType.MESH
 F32 = jnp.float32
 BF16 = jnp.bfloat16
@@ -16,12 +17,13 @@
 
 
 def kernel(
-    frames, hidden, cell_in, gate_bias, bias1, bias2, w_in, w_hid, w_first, w_second,
+    frames_hbm, hidden_hbm, cell_hbm, gate_bias_hbm, bias1_hbm, bias2_hbm, w_in, w_hid, w_first, w_second,
     decoded, cell_out,
+    frames, hidden, cell_in, gate_bias, bias1, bias2,
     packed, packed_cell, own, edge_top, edge_bot, image, halo_top, halo_bot,
-    far_top_out, far_bot_out, far_top, far_bot,
+    far_top_out, far_bot_out, far_top, far_bot, frame_top, frame_bot,
     wi, wh, w1, w2, bias_col, cell, gin, dec_out, dec_in, cell_back,
-    w_sem, wx_send, wx_recv, s1_send, s1_recv, c1_send, c1_recv, local_sem,
+    in_sem, w_sem, wx_send, wx_recv, s_send, s_recv, f_send, f_recv,
     x_send, x_recv, ht_send, ht_recv, hb_send, hb_recv, fin_send, fin_recv, c2_send, c2_recv, d_send, d_recv,
 ):
     patch = lax.axis_index("patch")
@@ -45,10 +47,34 @@
     has_up = block > 0
     has_down = block < 7
     sibling = (patch, grp * 2 + 1 - core)
+    z = lax.rem(grp, 4)
+    group_patch = [holder(block, g, 0)[0] for g in (0, 4)]
+    up_patch = [holder(block - 1, g, 0)[0] for g in (0, 4)]
+    down_patch = [holder(block + 1, g, 0)[0] for g in (0, 4)]
+    cross_patch = jnp.where(x_hi == 0, group_patch[1], group_patch[0])
 
     def peer(d):
-        g = lax.rem(grp // 4 + d // 4, 2) * 4 + lax.rem(lax.rem(grp, 4) + lax.rem(d, 4), 4)
-        return g
+        hi = 1 - x_hi if d >= 4 else x_hi
+        return (cross_patch if d >= 4 else patch, (hi * 4 + lax.rem(z + d % 4, 4)) * 2 + core)
+
+    above_same = (jnp.where(x_hi == 0, up_patch[0], up_patch[1]), hid)
+    below_same = (jnp.where(x_hi == 0, down_patch[0], down_patch[1]), hid)
+
+    def above(g):
+        return (up_patch[g // 4], g * 2 + core)
+
+    def below(g):
+        return (down_patch[g // 4], g * 2 + core)
+
+    in_copies = []
+    loads = (
+        (frames_hbm, frames), (hidden_hbm, hidden), (cell_hbm, cell_in),
+        (gate_bias_hbm, gate_bias), (bias1_hbm, bias1), (bias2_hbm, bias2),
+    )
+    for k, (src, dst) in enumerate(loads):
+        copy = pltpu.make_async_copy(src, dst, in_sem.at[k])
+        copy.start()
+        in_copies.append(copy)
 
     barrier = pltpu.get_barrier_semaphore()
 
@@ -62,19 +88,18 @@
         greet(trade(0))
         greet(trade(1))
 
-    @pl.loop(1, 8)
-    def _(d):
-        greet(holder(block, peer(d), core))
-
-    @pl.loop(0, 8)
-    def _(g):
-        @pl.when(has_up)
-        def _():
-            greet(holder(block - 1, g, core))
-
-        @pl.when(has_down)
-        def _():
-            greet(holder(block + 1, g, core))
+    for d in FAR_FIRST:
+        greet(peer(d))
+
+    @pl.when(has_up)
+    def _():
+        for g in range(8):
+            greet(above(g))
+
+    @pl.when(has_down)
+    def _():
+        for g in range(8):
+            greet(below(g))
 
     weight_copies = []
     for k, (src, dst) in enumerate(((w_in, wi), (w_hid, wh))):
@@ -86,10 +111,12 @@
         copy.start()
         weight_copies.append(copy)
 
+    for copy in in_copies:
+        copy.wait()
     for b in range(2):
+        packed[b, 0] = jnp.concatenate([hidden[b, r] for r in (0, 2, 1, 3)], axis=-1)
         for t in range(STEPS):
-            packed[b, t] = jnp.concatenate([frames[t, b, r] for r in (0, 2, 1, 3)], axis=-1)
-        packed[b, STEPS] = jnp.concatenate([hidden[b, r] for r in (0, 2, 1, 3)], axis=-1)
+            packed[b, 1 + t] = jnp.concatenate([frames[t, b, r] for r in (0, 2, 1, 3)], axis=-1)
         packed_cell[b] = jnp.concatenate([cell_in[b, r] for r in (0, 2, 1, 3)], axis=-1)
     eye = lax.broadcasted_iota(jnp.int32, (32, 32), 0) == lax.broadcasted_iota(jnp.int32, (32, 32), 1)
     for k in range(4):
@@ -111,36 +138,41 @@
 
     my_rows = pl.ds(pl.multiple_of(core * 32, 32), 32)
 
-    def trade_copies(c, b, rows):
-        return (
-            pltpu.make_async_remote_copy(
-                src_ref=packed.at[b], dst_ref=own.at[0 : STEPS + 1, rows, :],
-                send_sem=s1_send.at[b], recv_sem=s1_recv.at[c],
-                device_id=trade(b), device_id_type=MESH,
-            ),
-            pltpu.make_async_remote_copy(
-                src_ref=packed_cell.at[b], dst_ref=cell.at[c],
-                send_sem=c1_send.at[b], recv_sem=c1_recv.at[c],
-                device_id=trade(b), device_id_type=MESH,
-            ),
+    def trade_copy(k, c, b, rows):
+        src, dst = (
+            (lambda: (packed.at[b, 0:2], own.at[1:3, rows, :])),
+            (lambda: (packed.at[b, 2:5], own.at[3:6, rows, :])),
+            (lambda: (packed_cell.at[b], cell.at[c])),
+        )[k]()
+        return pltpu.make_async_remote_copy(
+            src_ref=src, dst_ref=dst, send_sem=s_send.at[k, b], recv_sem=s_recv.at[k, c],
+            device_id=trade(b), device_id_type=MESH,
         )
 
-    for b in range(2):
-        stays = (flip == 0) & (core == b)
-
-        @pl.when(jnp.logical_not(stays))
-        def _(b=b):
-            for copy in trade_copies(core, b, my_rows):
-                copy.start()
-
-        @pl.when(stays)
-        def _(b=b):
-            one = pltpu.make_async_copy(packed.at[b], own.at[0 : STEPS + 1, my_rows, :], local_sem.at[0])
-            two = pltpu.make_async_copy(packed_cell.at[b], cell.at[core], local_sem.at[1])
-            one.start()
-            two.start()
-            one.wait()
-            two.wait()
+    def start_trades(kinds):
+        for b in range(2):
+            stays = (flip == 0) & (core == b)
+
+            @pl.when(jnp.logical_not(stays))
+            def _(b=b):
+                for k in kinds:
+                    trade_copy(k, core, b, my_rows).start()
+
+    def wait_trades(kinds):
+        for c in range(2):
+            stays = (flip == 0) & (core == c)
+
+            @pl.when(jnp.logical_not(stays))
+            def _(c=c):
+                for k in kinds:
+                    trade_copy(k, c, 0, pl.ds(c * 32, 32)).wait_recv()
+
+    start_trades((0,))
+
+    @pl.when(flip == 0)
+    def _():
+        own[1:6, my_rows, :] = packed[core]
+        cell[core] = packed_cell[core]
 
     def weight_trade(k, src, dst):
         return pltpu.make_async_remote_copy(
@@ -155,14 +187,7 @@
     ]
     for copy in trades:
         copy.start()
-
-    for c in range(2):
-        stays = (flip == 0) & (core == c)
-
-        @pl.when(jnp.logical_not(stays))
-        def _(c=c):
-            for copy in trade_copies(c, 0, pl.ds(c * 32, 32)):
-                copy.wait_recv()
+    wait_trades((0,))
 
     half = lax.broadcasted_iota(jnp.int32, (32, 128), 1) < 64
     my_tile = pl.ds(pl.multiple_of(grp * 64, 64), 64)
@@ -174,69 +199,84 @@
         edge_top[slot] = jnp.where(half, a[:32], swap_halves(a[32:]))
         edge_bot[slot] = jnp.where(half, swap_halves(b[:32]), b[32:])
 
-    def tile_copy(slot, d):
-        return pltpu.make_async_remote_copy(
-            src_ref=own.at[slot], dst_ref=image.at[slot, my_tile, 128:384],
-            send_sem=x_send.at[slot], recv_sem=x_recv.at[slot],
-            device_id=holder(block, peer(d), core), device_id_type=MESH,
-        )
-
-    def up_copy(slot, g):
-        return pltpu.make_async_remote_copy(
-            src_ref=edge_top.at[slot], dst_ref=halo_bot.at[slot, my_edge, :],
-            send_sem=ht_send.at[slot], recv_sem=hb_recv.at[slot],
-            device_id=holder(block - 1, g, core), device_id_type=MESH,
-        )
-
-    def down_copy(slot, g):
-        return pltpu.make_async_remote_copy(
-            src_ref=edge_bot.at[slot], dst_ref=halo_top.at[slot, my_edge, :],
-            send_sem=hb_send.at[slot], recv_sem=ht_recv.at[slot],
-            device_id=holder(block + 1, g, core), device_id_type=MESH,
-        )
-
-    def send_tiles(slot):
+    def wait_bytes(ref, sem):
+        pltpu.make_async_copy(ref, ref, sem).wait()
+
+    def send(src, dst, send_sem, recv_sem, device):
+        pltpu.make_async_remote_copy(
+            src_ref=src, dst_ref=dst, send_sem=send_sem, recv_sem=recv_sem, device_id=device, device_id_type=MESH
+        ).start()
+
+    def send_tiles(slot, distances):
+        for d in distances:
+            send(own.at[slot], image.at[slot, my_tile, 128:384], x_send.at[slot], x_recv.at[slot], peer(d))
         image[slot, my_tile, 128:384] = own[slot]
-
-        @pl.loop(1, 8)
-        def _(k):
-            tile_copy(slot, 8 - k).start()
 
     def broadcast(slot):
         pack_edges(slot)
 
-        @pl.loop(0, 8)
-        def _(g):
-            @pl.when(has_up)
-            def _():
-                up_copy(slot, g).start()
-
-            @pl.when(has_down)
-            def _():
-                down_copy(slot, g).start()
-
-        send_tiles(slot)
-
-    def wait_bytes(ref, sem):
-        pltpu.make_async_copy(ref, ref, sem).wait()
+        @pl.when(has_up)
+        def _():
+            for g in range(8):
+                send(edge_top.at[slot], halo_bot.at[slot, my_edge, :], ht_send.at[slot], hb_recv.at[slot], above(g))
+
+        @pl.when(has_down)
+        def _():
+            for g in range(8):
+                send(edge_bot.at[slot], halo_top.at[slot, my_edge, :], hb_send.at[slot], ht_recv.at[slot], below(g))
+
+        send_tiles(slot, FAR_FIRST)
 
     def wait_tiles(slot):
         wait_bytes(image.at[slot, 0:448, 128:384], x_recv.at[slot])
 
+    def wait_edges_sent(slot):
+        @pl.when(has_up)
+        def _():
+            wait_bytes(halo_top.at[slot], ht_send.at[slot])
+
+        @pl.when(has_down)
+        def _():
+            wait_bytes(halo_bot.at[slot], hb_send.at[slot])
+
     def wait_sent(slot):
         wait_bytes(image.at[slot, 0:448, 128:384], x_send.at[slot])
+        wait_edges_sent(slot)
+
+    my_half = pl.ds(pl.multiple_of(x_hi * 256, 256), 256)
+
+    def frame_along_z(t):
+        send_tiles(2 + t, (2, 1, 3))
+
+    def frame_along_x(t):
+        slot = 2 + t
+        wait_bytes(image.at[slot, 0:192, 128:384], x_recv.at[slot])
+        block_ref = image.at[slot, my_half, 128:384]
+        send(block_ref, block_ref, f_send.at[t], f_recv.at[t], peer(4))
+
+    def frame_edges(t):
+        slot = 2 + t
+        wait_bytes(image.at[slot, 0:256, 128:384], f_recv.at[t])
+        for g in range(8):
+            first = slice(g * 64, g * 64 + 32)
+            later = slice(g * 64 + 32, g * 64 + 64)
+            packed_rows = slice(g * 32, g * 32 + 32)
+            frame_top[t, packed_rows] = jnp.where(
+                half, image[slot, first, 128:256], swap_halves(image[slot, later, 128:256])
+            )
+            frame_bot[t, packed_rows] = jnp.where(
+                half, swap_halves(image[slot, first, 256:384]), image[slot, later, 256:384]
+            )
 
         @pl.when(has_up)
         def _():
-            wait_bytes(halo_top.at[slot], ht_send.at[slot])
+            send(frame_top.at[t], halo_bot.at[slot], ht_send.at[slot], hb_recv.at[slot], above_same)
 
         @pl.when(has_down)
         def _():
-            wait_bytes(halo_bot.at[slot], hb_send.at[slot])
-
-    def wait_image(slot):
-        wait_tiles(slot)
-
+            send(frame_bot.at[t], halo_top.at[slot], hb_send.at[slot], ht_recv.at[slot], below_same)
+
+    def wait_halos(slot):
         @pl.when(has_up)
         def _():
             wait_bytes(halo_top.at[slot], ht_recv.at[slot])
@@ -260,25 +300,31 @@
     place = lax.rem(lax.broadcasted_iota(jnp.int32, (256, 128), 1), 64)
 
     def conv(slot, weight, write):
-        parts = []
-        for q in range(3):
-            total = None
-            for p in range(3):
-                lhs = weight[p, q].reshape(256, 512)
-                term = jnp.dot(lhs, image[slot, :, p * 128 : p * 128 + 256], preferred_element_type=F32)
-                total = term if total is None else total + term
-            parts.append(total)
+        def tap(p, q):
+            lhs = weight[p, q].reshape(256, 512)
+            return jnp.dot(lhs, image[slot, :, p * 128 : p * 128 + 256], preferred_element_type=F32)
+
+        parts = [tap(1, q) for q in range(3)]
+        wait_halos(slot)
+        parts = [parts[q] + tap(0, q) + tap(2, q) for q in range(3)]
         for tile in range(2):
             lanes = slice(tile * 128, (tile + 1) * 128)
             left = jnp.where(place == 0, 0.0, pltpu.roll(parts[0][:, lanes], 1, 1))
             right = jnp.where(place == 63, 0.0, pltpu.roll(parts[2][:, lanes], 127, 1))
             write(lanes, parts[1][:, lanes] + left + right)
 
-    broadcast(0)
-    broadcast(STEPS)
+    broadcast(1)
+    frame_along_z(0)
+    start_trades((1, 2))
+    frame_along_x(0)
+    wait_trades((1, 2))
+    frame_along_z(1)
+    frame_edges(0)
+    frame_along_z(2)
+    frame_along_x(1)
     weight_copies[0].wait()
     weight_copies[1].wait()
-    for k, copy in enumerate(trades):
+    for copy in trades:
         copy.wait_recv()
 
     def write_gin(lanes, value):
@@ -298,21 +344,28 @@
         return write
 
     def step(t, carry):
-        slot = STEPS + lax.rem(t, 2)
-        following = STEPS + lax.rem(t + 1, 2)
+        slot = lax.rem(t + 1, 2)
+        following = lax.rem(t, 2)
+
+        @pl.when(t < STEPS - 3)
+        def _():
+            frame_along_z(t + 3)
+
+        @pl.when(t < STEPS - 2)
+        def _():
+            frame_along_x(t + 2)
 
         @pl.when(t < STEPS - 1)
         def _():
-            broadcast(t + 1)
-
-        wait_image(t)
-        conv(t, wi, write_gin)
-        wait_image(slot)
+            frame_edges(t + 1)
+
+        conv(2 + t, wi, write_gin)
 
         @pl.when(t > 0)
         def _():
             wait_sent(following)
 
+        wait_tiles(slot)
         conv(slot, wh, update(following))
 
         @pl.when(t < STEPS - 1)
@@ -323,38 +376,24 @@
 
     lax.fori_loop(0, STEPS, step, 0)
 
-    last = STEPS + STEPS % 2
+    last = (STEPS + 1) % 2
     wide = lax.broadcasted_iota(jnp.int32, (64, 128), 1) < 64
     row_a = own[last, :, 0:128]
     row_b = own[last, :, 128:256]
     far_top_out[...] = jnp.where(wide, row_a, swap_halves(row_b))
     far_bot_out[...] = jnp.where(wide, swap_halves(row_a), row_b)
 
-    def far_up_copy(g):
-        return pltpu.make_async_remote_copy(
-            src_ref=far_top_out, dst_ref=far_bot.at[my_tile, :],
-            send_sem=fin_send.at[0], recv_sem=fin_recv.at[0],
-            device_id=holder(block - 1, g, core), device_id_type=MESH,
-        )
-
-    def far_down_copy(g):
-        return pltpu.make_async_remote_copy(
-            src_ref=far_bot_out, dst_ref=far_top.at[my_tile, :],
-            send_sem=fin_send.at[1], recv_sem=fin_recv.at[1],
-            device_id=holder(block + 1, g, core), device_id_type=MESH,
-        )
-
-    @pl.loop(0, 8)
-    def _(g):
-        @pl.when(has_up)
-        def _():
-            far_up_copy(g).start()
-
-        @pl.when(has_down)
-        def _():
-            far_down_copy(g).start()
-
-    send_tiles(last)
+    @pl.when(has_up)
+    def _():
+        for g in range(8):
+            send(far_top_out, far_bot.at[my_tile, :], fin_send.at[0], fin_recv.at[0], above(g))
+
+    @pl.when(has_down)
+    def _():
+        for g in range(8):
+            send(far_bot_out, far_top.at[my_tile, :], fin_send.at[1], fin_recv.at[1], below(g))
+
+    send_tiles(last, FAR_FIRST)
 
     def cell_copy(c, b):
         return pltpu.make_async_remote_copy(
@@ -372,9 +411,7 @@
 
         @pl.when(stays)
         def _(c=c):
-            copy = pltpu.make_async_copy(cell.at[c], cell_back.at[core], local_sem.at[1])
-            copy.start()
-            copy.wait()
+            cell_back[core] = cell[c]
 
     weight_copies[2].wait()
     weight_copies[3].wait()
@@ -454,9 +491,11 @@
             start = (r % 2) * 128 + (r // 2) * 64
             cell_out[b, r] = cell_back[b, :, start : start + 64]
 
-    for slot in range(STEPS):
-        wait_sent(slot)
-    wait_sent(STEPS + 1)
+    for t in range(STEPS):
+        wait_bytes(image.at[2 + t, 0:192, 128:384], x_send.at[2 + t])
+        wait_bytes(image.at[2 + t, 0:256, 128:384], f_send.at[t])
+        wait_edges_sent(2 + t)
+    wait_sent(1 - last)
     wait_bytes(image.at[last, 0:448, 128:384], x_send.at[last])
 
     @pl.when(has_up)
@@ -475,8 +514,8 @@
 
         @pl.when(jnp.logical_not(stays))
         def _(b=b):
-            for copy in trade_copies(core, b, my_rows):
-                copy.wait_send()
+            for k in range(3):
+                trade_copy(k, core, b, my_rows).wait_send()
             cell_copy(b, core).wait_send()
             dec_copy(0, b).wait_recv()
             dec_copy(b, core).wait_send()
@@ -489,13 +528,25 @@
     first_weight, first_bias, second_weight, second_bias,
 ):
     vmem = pl.BlockSpec(memory_space=pltpu.VMEM)
-    anywhere = pl.BlockSpec(memory_space=pl.ANY)
+    hbm = pl.BlockSpec(memory_space=pltpu.HBM)
     dma = pltpu.SemaphoreType.DMA
     slots = STEPS + 2
 
     def gate_rows(weight):
         return weight.transpose(0, 1, 3, 4, 2).reshape(3, 3, 128, 512)
 
+    operands = (
+        frames.transpose(0, 1, 2, 4, 3),
+        hidden_start.transpose(0, 1, 3, 2),
+        cell_start.transpose(0, 1, 3, 2),
+        gate_bias,
+        first_bias.reshape(1, -1),
+        second_bias.reshape(1, -1),
+        gate_rows(input_weight),
+        gate_rows(hidden_weight),
+        first_weight,
+        second_weight,
+    )
     decoded, cell = pl.pallas_call(
         kernel,
         name="convlstm",
@@ -503,14 +554,20 @@
             jax.ShapeDtypeStruct((2, 4, 4, 512), BF16),
             jax.ShapeDtypeStruct((2, 4, 32, 64), F32),
         ),
-        in_specs=[vmem] * 6 + [anywhere] * 4,
+        in_specs=[hbm] * 10,
         out_specs=(vmem, vmem),
         scratch_shapes=[
+            pltpu.VMEM((STEPS, 2, 4, 32, 64), BF16),
+            pltpu.VMEM((2, 4, 32, 64), BF16),
+            pltpu.VMEM((2, 4, 32, 64), F32),
+            pltpu.VMEM((4, 32), F32),
+            pltpu.VMEM((1, 512), F32),
+            pltpu.VMEM((1, 512), F32),
             pltpu.VMEM((2, STEPS + 1, 32, 256), BF16),
             pltpu.VMEM((2, 32, 256), F32),
             pltpu.VMEM((slots, 64, 256), BF16),
-            pltpu.VMEM((slots, 32, 128), BF16),
-            pltpu.VMEM((slots, 32, 128), BF16),
+            pltpu.VMEM((2, 32, 128), BF16),
+            pltpu.VMEM((2, 32, 128), BF16),
             pltpu.VMEM((slots, 512, 512), BF16),
             pltpu.VMEM((slots, 256, 128), BF16),
             pltpu.VMEM((slots, 256, 128), BF16),
@@ -518,6 +575,8 @@
             pltpu.VMEM((64, 128), BF16),
             pltpu.VMEM((512, 128), BF16),
             pltpu.VMEM((512, 128), BF16),
+            pltpu.VMEM((STEPS, 256, 128), BF16),
+            pltpu.VMEM((STEPS, 256, 128), BF16),
             pltpu.VMEM((3, 3, 2, 128, 512), BF16),
             pltpu.VMEM((3, 3, 2, 128, 512), BF16),
             pltpu.VMEM((3, 3, 512, 512), BF16),
@@ -528,7 +587,7 @@
             pltpu.VMEM((2, 4, 4, 512), BF16),
             pltpu.VMEM((2, 4, 4, 512), BF16),
             pltpu.VMEM((2, 32, 256), F32),
-            dma((4,)), dma((3,)), dma((3,)), dma((2,)), dma((2,)), dma((2,)), dma((2,)), dma((2,)),
+            dma((6,)), dma((4,)), dma((3,)), dma((3,)), dma((3, 2)), dma((3, 2)), dma((STEPS,)), dma((STEPS,)),
             dma((slots,)), dma((slots,)), dma((slots,)), dma((slots,)), dma((slots,)), dma((slots,)),
             dma((2,)), dma((2,)), dma((2,)), dma((2,)), dma((2,)), dma((2,)),
         ],
@@ -536,16 +595,7 @@
             collective_id=0, has_side_effects=True, vmem_limit_bytes=50 << 20
         ),
     )(
-        frames.transpose(0, 1, 2, 4, 3),
-        hidden_start.transpose(0, 1, 3, 2),
-        cell_start.transpose(0, 1, 3, 2),
-        gate_bias,
-        first_bias.reshape(1, -1),
-        second_bias.reshape(1, -1),
-        gate_rows(input_weight),
-        gate_rows(hidden_weight),
-        first_weight,
-        second_weight,
+        *(pltpu.with_memory_space_constraint(array, pltpu.HBM) for array in operands)
     )
     return decoded, cell.transpose(0, 1, 3, 2)
 

time: 75.5 us -> 65.3 us (0.86)
  local copies, waits for them, and re-layouts: 8.54 us -> 1.27 us
  Pallas kernels: 65.9 us -> 63.2 us
    unnamed x18 -> x2, local copies, waits for them, and re-layouts: 8.54 us -> 1.27 us
    pallas_call x1, Pallas kernels: 65.9 us -> 63.2 us  [per_device(): pl.pallas_call(kernel, name='convlstm', out_shape=(jax.ShapeDtypeStruct((...]
where the time goes in v2:
time: 65.3 us; the launch traced here: 65.2 us
  Pallas kernels  63.2 us (97%)
  local copies, waits for them, and re-layouts  1.27 us (2%)
    pallas_call x1, Pallas kernels, per_device(): pl.pallas_call(kernel, name='convlstm', out_shape=(jax.ShapeDtypeStruct((...  63.2 us

profile of v2, /device:TPU:11, one launch (start us, length us, event | category | flops | bytes accessed | tf_op | source)
XLA Modules:
  0.0 65.2 jit_solution(918887128528461081)
XLA Ops:
  0.6 63.2 %convlstm.1 = (bf16[2,4,4,512]{3,2,1,0:T(4,128)(2,1)S(1)}, f32[2,4,32,64]{3,2,1,0:T(8,128)S(1)}) custom-call(bf16[4,2,4,32,64]{4,3,2,1,0:T(8,128)(2,1)} %bitcast.15, bf16[2,4,32,64]{3,2,1,0:T(8,128)(2,1)} %bitcast.17, f32[2,4,32,64]{3,2,1,0:T(8,128)} %bitcast.16, f32[4,32]{1,0:T(4,128)} %gate_bias_hbm.1, f32[1,512]{1,0:T(1,128)} %bitcast.18, ...), custom_call_target="tpu_custom_call" | custom-call | tf_op jit(solution)/shard_map/convlstm/pallas_call | solution.py:550
  63.9 0.6 copy.14
  64.5 0.7 %copy.15 = f32[2,4,64,32]{2,3,1,0:T(8,128)} copy(f32[2,4,64,32]{2,3,1,0:T(8,128)S(1)} %bitcast.12) | data formatting | bytes 131072

commit v3 on v2

--- a/solution.py
+++ b/solution.py
@@ -7,6 +7,7 @@
 
 STEPS = 4
 FAR_FIRST = (6, 5, 7, 2, 4, 1, 3)
+FAR_Z = (2, 1, 3, 0)
 MESH = pl.DeviceIdType.MESH
 F32 = jnp.float32
 BF16 = jnp.bfloat16
@@ -57,14 +58,11 @@
         hi = 1 - x_hi if d >= 4 else x_hi
         return (cross_patch if d >= 4 else patch, (hi * 4 + lax.rem(z + d % 4, 4)) * 2 + core)
 
-    above_same = (jnp.where(x_hi == 0, up_patch[0], up_patch[1]), hid)
-    below_same = (jnp.where(x_hi == 0, down_patch[0], down_patch[1]), hid)
-
-    def above(g):
-        return (up_patch[g // 4], g * 2 + core)
-
-    def below(g):
-        return (down_patch[g // 4], g * 2 + core)
+    def above(k):
+        return (up_patch[k % 2], (k % 2 * 4 + lax.rem(z + FAR_Z[k // 2], 4)) * 2 + core)
+
+    def below(k):
+        return (down_patch[k % 2], (k % 2 * 4 + lax.rem(z + FAR_Z[k // 2], 4)) * 2 + core)
 
     in_copies = []
     loads = (
@@ -244,37 +242,32 @@
         wait_edges_sent(slot)
 
     my_half = pl.ds(pl.multiple_of(x_hi * 256, 256), 256)
+    my_edges = pl.ds(pl.multiple_of(x_hi * 128, 128), 128)
 
     def frame_along_z(t):
         send_tiles(2 + t, (2, 1, 3))
 
-    def frame_along_x(t):
+    def frame_onward(t):
         slot = 2 + t
         wait_bytes(image.at[slot, 0:192, 128:384], x_recv.at[slot])
         block_ref = image.at[slot, my_half, 128:384]
         send(block_ref, block_ref, f_send.at[t], f_recv.at[t], peer(4))
-
-    def frame_edges(t):
-        slot = 2 + t
-        wait_bytes(image.at[slot, 0:256, 128:384], f_recv.at[t])
-        for g in range(8):
-            first = slice(g * 64, g * 64 + 32)
-            later = slice(g * 64 + 32, g * 64 + 64)
-            packed_rows = slice(g * 32, g * 32 + 32)
-            frame_top[t, packed_rows] = jnp.where(
-                half, image[slot, first, 128:256], swap_halves(image[slot, later, 128:256])
-            )
-            frame_bot[t, packed_rows] = jnp.where(
-                half, swap_halves(image[slot, first, 256:384]), image[slot, later, 256:384]
-            )
+        for k in range(4):
+            first = pl.ds(pl.multiple_of(x_hi * 256 + k * 64, 64), 32)
+            later = pl.ds(pl.multiple_of(x_hi * 256 + k * 64 + 32, 32), 32)
+            rows = slice(k * 32, k * 32 + 32)
+            frame_top[t, rows] = jnp.where(half, image[slot, first, 128:256], swap_halves(image[slot, later, 128:256]))
+            frame_bot[t, rows] = jnp.where(half, swap_halves(image[slot, first, 256:384]), image[slot, later, 256:384])
 
         @pl.when(has_up)
         def _():
-            send(frame_top.at[t], halo_bot.at[slot], ht_send.at[slot], hb_recv.at[slot], above_same)
+            for k in (6, 7):
+                send(frame_top.at[t], halo_bot.at[slot, my_edges, :], ht_send.at[slot], hb_recv.at[slot], above(k))
 
         @pl.when(has_down)
         def _():
-            send(frame_bot.at[t], halo_top.at[slot], hb_send.at[slot], ht_recv.at[slot], below_same)
+            for k in (6, 7):
+                send(frame_bot.at[t], halo_top.at[slot, my_edges, :], hb_send.at[slot], ht_recv.at[slot], below(k))
 
     def wait_halos(slot):
         @pl.when(has_up)
@@ -313,15 +306,12 @@
             right = jnp.where(place == 63, 0.0, pltpu.roll(parts[2][:, lanes], 127, 1))
             write(lanes, parts[1][:, lanes] + left + right)
 
+    frame_along_z(0)
     broadcast(1)
-    frame_along_z(0)
     start_trades((1, 2))
-    frame_along_x(0)
+    frame_onward(0)
     wait_trades((1, 2))
     frame_along_z(1)
-    frame_edges(0)
-    frame_along_z(2)
-    frame_along_x(1)
     weight_copies[0].wait()
     weight_copies[1].wait()
     for copy in trades:
@@ -347,18 +337,7 @@
         slot = lax.rem(t + 1, 2)
         following = lax.rem(t, 2)
 
-        @pl.when(t < STEPS - 3)
-        def _():
-            frame_along_z(t + 3)
-
-        @pl.when(t < STEPS - 2)
-        def _():
-            frame_along_x(t + 2)
-
-        @pl.when(t < STEPS - 1)
-        def _():
-            frame_edges(t + 1)
-
+        wait_bytes(image.at[2 + t, 0:256, 128:384], f_recv.at[t])
         conv(2 + t, wi, write_gin)
 
         @pl.when(t > 0)
@@ -371,6 +350,11 @@
         @pl.when(t < STEPS - 1)
         def _():
             broadcast(following)
+            frame_onward(t + 1)
+
+        @pl.when(t < STEPS - 2)
+        def _():
+            frame_along_z(t + 2)
 
         return carry
 
@@ -575,8 +559,8 @@
             pltpu.VMEM((64, 128), BF16),
             pltpu.VMEM((512, 128), BF16),
             pltpu.VMEM((512, 128), BF16),
-            pltpu.VMEM((STEPS, 256, 128), BF16),
-            pltpu.VMEM((STEPS, 256, 128), BF16),
+            pltpu.VMEM((STEPS, 128, 128), BF16),
+            pltpu.VMEM((STEPS, 128, 128), BF16),
             pltpu.VMEM((3, 3, 2, 128, 512), BF16),
             pltpu.VMEM((3, 3, 2, 128, 512), BF16),
             pltpu.VMEM((3, 3, 512, 512), BF16),

time: 65.3 us -> 74.2 us (1.14)
  Pallas kernels: 63.2 us -> 72.2 us
    pallas_call x1, Pallas kernels: 63.2 us -> 72.2 us  [per_device(): pl.pallas_call(kernel, name='convlstm', out_shape=(jax.ShapeDtypeStruct((...]
where the time goes in v3:
time: 74.2 us; the launch traced here: 74.1 us
  Pallas kernels  72.2 us (97%)
  local copies, waits for them, and re-layouts  1.27 us (2%)
    pallas_call x1, Pallas kernels, per_device(): pl.pallas_call(kernel, name='convlstm', out_shape=(jax.ShapeDtypeStruct((...  72.2 us

profile of v3, /device:TPU:11, one launch (start us, length us, event | category | flops | bytes accessed | tf_op | source)
XLA Modules:
  0.0 74.1 jit_solution(7877021145252733601)
XLA Ops:
  0.6 72.2 %convlstm.1 = (bf16[2,4,4,512]{3,2,1,0:T(4,128)(2,1)S(1)}, f32[2,4,32,64]{3,2,1,0:T(8,128)S(1)}) custom-call(bf16[4,2,4,32,64]{4,3,2,1,0:T(8,128)(2,1)} %bitcast.15, bf16[2,4,32,64]{3,2,1,0:T(8,128)(2,1)} %bitcast.17, f32[2,4,32,64]{3,2,1,0:T(8,128)} %bitcast.16, f32[4,32]{1,0:T(4,128)} %gate_bias_hbm.1, f32[1,512]{1,0:T(1,128)} %bitcast.18, ...), custom_call_target="tpu_custom_call" | custom-call | tf_op jit(solution)/shard_map/convlstm/pallas_call | solution.py:534
  72.9 0.6 copy.14
  73.5 0.7 copy.15

commit v4 on v2

--- a/solution.py
+++ b/solution.py
@@ -7,6 +7,7 @@
 
 STEPS = 4
 FAR_FIRST = (6, 5, 7, 2, 4, 1, 3)
+FAR_Z = (2, 1, 3, 0)
 MESH = pl.DeviceIdType.MESH
 F32 = jnp.float32
 BF16 = jnp.bfloat16
@@ -60,11 +61,11 @@
     above_same = (jnp.where(x_hi == 0, up_patch[0], up_patch[1]), hid)
     below_same = (jnp.where(x_hi == 0, down_patch[0], down_patch[1]), hid)
 
-    def above(g):
-        return (up_patch[g // 4], g * 2 + core)
-
-    def below(g):
-        return (down_patch[g // 4], g * 2 + core)
+    def above(k):
+        return (up_patch[k % 2], (k % 2 * 4 + lax.rem(z + FAR_Z[k // 2], 4)) * 2 + core)
+
+    def below(k):
+        return (down_patch[k % 2], (k % 2 * 4 + lax.rem(z + FAR_Z[k // 2], 4)) * 2 + core)
 
     in_copies = []
     loads = (
@@ -114,9 +115,10 @@
     for copy in in_copies:
         copy.wait()
     for b in range(2):
-        packed[b, 0] = jnp.concatenate([hidden[b, r] for r in (0, 2, 1, 3)], axis=-1)
-        for t in range(STEPS):
-            packed[b, 1 + t] = jnp.concatenate([frames[t, b, r] for r in (0, 2, 1, 3)], axis=-1)
+        for i in range(2):
+            packed[b, 0, i] = jnp.concatenate([hidden[b, i], hidden[b, i + 2]], axis=-1)
+            for t in range(STEPS):
+                packed[b, 1 + t, i] = jnp.concatenate([frames[t, b, i], frames[t, b, i + 2]], axis=-1)
         packed_cell[b] = jnp.concatenate([cell_in[b, r] for r in (0, 2, 1, 3)], axis=-1)
     eye = lax.broadcasted_iota(jnp.int32, (32, 32), 0) == lax.broadcasted_iota(jnp.int32, (32, 32), 1)
     for k in range(4):
@@ -140,8 +142,8 @@
 
     def trade_copy(k, c, b, rows):
         src, dst = (
-            (lambda: (packed.at[b, 0:2], own.at[1:3, rows, :])),
-            (lambda: (packed.at[b, 2:5], own.at[3:6, rows, :])),
+            (lambda: (packed.at[b, 0:2], own.at[1:3, :, rows, :])),
+            (lambda: (packed.at[b, 2:5], own.at[3:6, :, rows, :])),
             (lambda: (packed_cell.at[b], cell.at[c])),
         )[k]()
         return pltpu.make_async_remote_copy(
@@ -171,7 +173,7 @@
 
     @pl.when(flip == 0)
     def _():
-        own[1:6, my_rows, :] = packed[core]
+        own[1:6, :, my_rows, :] = packed[core]
         cell[core] = packed_cell[core]
 
     def weight_trade(k, src, dst):
@@ -194,8 +196,8 @@
     my_edge = pl.ds(pl.multiple_of(grp * 32, 32), 32)
 
     def pack_edges(slot):
-        a = own[slot, :, 0:128]
-        b = own[slot, :, 128:256]
+        a = own[slot, 0]
+        b = own[slot, 1]
         edge_top[slot] = jnp.where(half, a[:32], swap_halves(a[32:]))
         edge_bot[slot] = jnp.where(half, swap_halves(b[:32]), b[32:])
 
@@ -209,10 +211,10 @@
 
     def send_tiles(slot, distances):
         for d in distances:
-            send(own.at[slot], image.at[slot, my_tile, 128:384], x_send.at[slot], x_recv.at[slot], peer(d))
-        image[slot, my_tile, 128:384] = own[slot]
-
-    def broadcast(slot):
+            send(own.at[slot], image.at[slot, 1:3, my_tile, :], x_send.at[slot], x_recv.at[slot], peer(d))
+        image[slot, 1:3, my_tile, :] = own[slot]
+
+    def send_edges(slot):
         pack_edges(slot)
 
         @pl.when(has_up)
@@ -225,10 +227,12 @@
             for g in range(8):
                 send(edge_bot.at[slot], halo_top.at[slot, my_edge, :], hb_send.at[slot], ht_recv.at[slot], below(g))
 
+    def broadcast(slot):
+        send_edges(slot)
         send_tiles(slot, FAR_FIRST)
 
     def wait_tiles(slot):
-        wait_bytes(image.at[slot, 0:448, 128:384], x_recv.at[slot])
+        wait_bytes(image.at[slot, 1:3, 0:448, :], x_recv.at[slot])
 
     def wait_edges_sent(slot):
         @pl.when(has_up)
@@ -240,33 +244,42 @@
             wait_bytes(halo_bot.at[slot], hb_send.at[slot])
 
     def wait_sent(slot):
-        wait_bytes(image.at[slot, 0:448, 128:384], x_send.at[slot])
+        wait_bytes(image.at[slot, 1:3, 0:448, :], x_send.at[slot])
         wait_edges_sent(slot)
 
     my_half = pl.ds(pl.multiple_of(x_hi * 256, 256), 256)
-
-    def frame_along_z(t):
-        send_tiles(2 + t, (2, 1, 3))
-
-    def frame_along_x(t):
+    cross_tile = pl.ds(pl.multiple_of((1 - x_hi) * 256 + z * 64, 64), 64)
+
+    def frame_first(t):
         slot = 2 + t
-        wait_bytes(image.at[slot, 0:192, 128:384], x_recv.at[slot])
-        block_ref = image.at[slot, my_half, 128:384]
-        send(block_ref, block_ref, f_send.at[t], f_recv.at[t], peer(4))
+        send(
+            own.at[slot, 1], image.at[slot, 2, my_tile, :], f_send.at[0, t], f_recv.at[0, t], peer(4)
+        )
+        send_tiles(slot, (2, 1, 3))
+
+    def frame_second(t):
+        slot = 2 + t
+        wait_bytes(image.at[slot, 2, 0:64, :], f_recv.at[0, t])
+        cross = image.at[slot, 2, cross_tile, :]
+        for d in (2, 1, 3):
+            send(cross, cross, f_send.at[1, t], f_recv.at[1, t], peer(d))
+        wait_bytes(image.at[slot, 1:3, 0:192, :], x_recv.at[slot])
+        half_ref = image.at[slot, 1, my_half, :]
+        send(half_ref, half_ref, f_send.at[2, t], f_recv.at[2, t], peer(4))
+
+    def frame_wait(t):
+        slot = 2 + t
+        wait_bytes(image.at[slot, 2, 0:192, :], f_recv.at[1, t])
+        wait_bytes(image.at[slot, 1, 0:256, :], f_recv.at[2, t])
 
     def frame_edges(t):
         slot = 2 + t
-        wait_bytes(image.at[slot, 0:256, 128:384], f_recv.at[t])
         for g in range(8):
             first = slice(g * 64, g * 64 + 32)
             later = slice(g * 64 + 32, g * 64 + 64)
-            packed_rows = slice(g * 32, g * 32 + 32)
-            frame_top[t, packed_rows] = jnp.where(
-                half, image[slot, first, 128:256], swap_halves(image[slot, later, 128:256])
-            )
-            frame_bot[t, packed_rows] = jnp.where(
-                half, swap_halves(image[slot, first, 256:384]), image[slot, later, 256:384]
-            )
+            rows = slice(g * 32, g * 32 + 32)
+            frame_top[t, rows] = jnp.where(half, image[slot, 1, first], swap_halves(image[slot, 1, later]))
+            frame_bot[t, rows] = jnp.where(half, swap_halves(image[slot, 2, first]), image[slot, 2, later])
 
         @pl.when(has_up)
         def _():
@@ -286,23 +299,24 @@
             wait_bytes(halo_bot.at[slot], hb_recv.at[slot])
 
         for g in range(8):
-            a0 = image[slot, g * 64 : g * 64 + 32, 128:256]
-            a1 = image[slot, g * 64 + 32 : g * 64 + 64, 128:256]
-            b0 = image[slot, g * 64 : g * 64 + 32, 256:384]
-            b1 = image[slot, g * 64 + 32 : g * 64 + 64, 256:384]
+            a0 = image[slot, 1, g * 64 : g * 64 + 32]
+            a1 = image[slot, 1, g * 64 + 32 : g * 64 + 64]
+            b0 = image[slot, 2, g * 64 : g * 64 + 32]
+            b1 = image[slot, 2, g * 64 + 32 : g * 64 + 64]
             top = halo_top[slot, g * 32 : g * 32 + 32, :]
             bot = halo_bot[slot, g * 32 : g * 32 + 32, :]
-            image[slot, g * 64 : g * 64 + 32, 0:128] = jnp.where(half, top, swap_halves(b0))
-            image[slot, g * 64 + 32 : g * 64 + 64, 0:128] = swap_halves(jnp.where(half, b1, top))
-            image[slot, g * 64 : g * 64 + 32, 384:512] = swap_halves(jnp.where(half, bot, a0))
-            image[slot, g * 64 + 32 : g * 64 + 64, 384:512] = jnp.where(half, swap_halves(a1), bot)
+            image[slot, 0, g * 64 : g * 64 + 32] = jnp.where(half, top, swap_halves(b0))
+            image[slot, 0, g * 64 + 32 : g * 64 + 64] = swap_halves(jnp.where(half, b1, top))
+            image[slot, 3, g * 64 : g * 64 + 32] = swap_halves(jnp.where(half, bot, a0))
+            image[slot, 3, g * 64 + 32 : g * 64 + 64] = jnp.where(half, swap_halves(a1), bot)
 
     place = lax.rem(lax.broadcasted_iota(jnp.int32, (256, 128), 1), 64)
 
     def conv(slot, weight, write):
         def tap(p, q):
             lhs = weight[p, q].reshape(256, 512)
-            return jnp.dot(lhs, image[slot, :, p * 128 : p * 128 + 256], preferred_element_type=F32)
+            rhs = jnp.concatenate([image[slot, p], image[slot, p + 1]], axis=1)
+            return jnp.dot(lhs, rhs, preferred_element_type=F32)
 
         parts = [tap(1, q) for q in range(3)]
         wait_halos(slot)
@@ -311,35 +325,34 @@
             lanes = slice(tile * 128, (tile + 1) * 128)
             left = jnp.where(place == 0, 0.0, pltpu.roll(parts[0][:, lanes], 1, 1))
             right = jnp.where(place == 63, 0.0, pltpu.roll(parts[2][:, lanes], 127, 1))
-            write(lanes, parts[1][:, lanes] + left + right)
-
+            write(tile, lanes, parts[1][:, lanes] + left + right)
+
+    frame_first(0)
     broadcast(1)
-    frame_along_z(0)
+    send_edges(2)
     start_trades((1, 2))
-    frame_along_x(0)
+    frame_second(0)
     wait_trades((1, 2))
-    frame_along_z(1)
-    frame_edges(0)
-    frame_along_z(2)
-    frame_along_x(1)
+    frame_first(1)
+    send_edges(3)
     weight_copies[0].wait()
     weight_copies[1].wait()
     for copy in trades:
         copy.wait_recv()
 
-    def write_gin(lanes, value):
+    def write_gin(tile, lanes, value):
         for c in range(2):
             rows = slice(c * 128, (c + 1) * 128)
             gin[rows, lanes] = value[rows] + bias_col[c]
 
     def update(next_slot):
-        def write(lanes, value):
+        def write(tile, lanes, value):
             gates = value + gin[:, lanes]
             for c in range(2):
                 z = [gates[c * 128 + k * 32 : c * 128 + (k + 1) * 32] for k in range(4)]
                 new = jax.nn.sigmoid(z[1] + 1.0) * cell[c, :, lanes] + jax.nn.sigmoid(z[0]) * jnp.tanh(z[2])
                 cell[c, :, lanes] = new
-                own[next_slot, c * 32 : (c + 1) * 32, lanes] = (jax.nn.sigmoid(z[3]) * jnp.tanh(new)).astype(BF16)
+                own[next_slot, tile, c * 32 : (c + 1) * 32] = (jax.nn.sigmoid(z[3]) * jnp.tanh(new)).astype(BF16)
 
         return write
 
@@ -347,19 +360,25 @@
         slot = lax.rem(t + 1, 2)
         following = lax.rem(t, 2)
 
-        @pl.when(t < STEPS - 3)
-        def _():
-            frame_along_z(t + 3)
+        frame_wait(t)
+
+        @pl.when(t > 1)
+        def _():
+            frame_edges(t)
+
+        @pl.when((t > 0) & (t < STEPS - 1))
+        def _():
+            frame_second(t + 1)
 
         @pl.when(t < STEPS - 2)
         def _():
-            frame_along_x(t + 2)
-
-        @pl.when(t < STEPS - 1)
-        def _():
-            frame_edges(t + 1)
+            frame_first(t + 2)
 
         conv(2 + t, wi, write_gin)
+
+        @pl.when(t == 0)
+        def _():
+            frame_second(t + 1)
 
         @pl.when(t > 0)
         def _():
@@ -378,8 +397,8 @@
 
     last = (STEPS + 1) % 2
     wide = lax.broadcasted_iota(jnp.int32, (64, 128), 1) < 64
-    row_a = own[last, :, 0:128]
-    row_b = own[last, :, 128:256]
+    row_a = own[last, 0]
+    row_b = own[last, 1]
     far_top_out[...] = jnp.where(wide, row_a, swap_halves(row_b))
     far_bot_out[...] = jnp.where(wide, swap_halves(row_a), row_b)
 
@@ -435,8 +454,8 @@
         return lax.dot_general(pick, tile, (((1,), (1,)), ((), ())), preferred_element_type=F32).astype(BF16)
 
     above = window(far_top[...])
-    tile_a = window(image[last, :, 128:256])
-    tile_b = window(image[last, :, 256:384])
+    tile_a = window(image[last, 1])
+    tile_b = window(image[last, 2])
     below = window(far_bot[...])
     pixels = jnp.concatenate([above, tile_a[:16], tile_b[:16], tile_a[16:], tile_b[16:], below], axis=0)
 
@@ -492,11 +511,13 @@
             cell_out[b, r] = cell_back[b, :, start : start + 64]
 
     for t in range(STEPS):
-        wait_bytes(image.at[2 + t, 0:192, 128:384], x_send.at[2 + t])
-        wait_bytes(image.at[2 + t, 0:256, 128:384], f_send.at[t])
+        wait_bytes(image.at[2 + t, 1:3, 0:192, :], x_send.at[2 + t])
+        wait_bytes(image.at[2 + t, 2, 0:64, :], f_send.at[0, t])
+        wait_bytes(image.at[2 + t, 2, 0:192, :], f_send.at[1, t])
+        wait_bytes(image.at[2 + t, 1, 0:256, :], f_send.at[2, t])
         wait_edges_sent(2 + t)
     wait_sent(1 - last)
-    wait_bytes(image.at[last, 0:448, 128:384], x_send.at[last])
+    wait_bytes(image.at[last, 1:3, 0:448, :], x_send.at[last])
 
     @pl.when(has_up)
     def _():
@@ -563,12 +584,12 @@
             pltpu.VMEM((4, 32), F32),
             pltpu.VMEM((1, 512), F32),
             pltpu.VMEM((1, 512), F32),
-            pltpu.VMEM((2, STEPS + 1, 32, 256), BF16),
+            pltpu.VMEM((2, STEPS + 1, 2, 32, 128), BF16),
             pltpu.VMEM((2, 32, 256), F32),
-            pltpu.VMEM((slots, 64, 256), BF16),
-            pltpu.VMEM((2, 32, 128), BF16),
-            pltpu.VMEM((2, 32, 128), BF16),
-            pltpu.VMEM((slots, 512, 512), BF16),
+            pltpu.VMEM((slots, 2, 64, 128), BF16),
+            pltpu.VMEM((4, 32, 128), BF16),
+            pltpu.VMEM((4, 32, 128), BF16),
+            pltpu.VMEM((slots, 4, 512, 128), BF16),
             pltpu.VMEM((slots, 256, 128), BF16),
             pltpu.VMEM((slots, 256, 128), BF16),
             pltpu.VMEM((64, 128), BF16),
@@ -587,7 +608,7 @@
             pltpu.VMEM((2, 4, 4, 512), BF16),
             pltpu.VMEM((2, 4, 4, 512), BF16),
             pltpu.VMEM((2, 32, 256), F32),
-            dma((6,)), dma((4,)), dma((3,)), dma((3,)), dma((3, 2)), dma((3, 2)), dma((STEPS,)), dma((STEPS,)),
+            dma((6,)), dma((4,)), dma((3,)), dma((3,)), dma((3, 2)), dma((3, 2)), dma((3, STEPS)), dma((3, STEPS)),
             dma((slots,)), dma((slots,)), dma((slots,)), dma((slots,)), dma((slots,)), dma((slots,)),
             dma((2,)), dma((2,)), dma((2,)), dma((2,)), dma((2,)), dma((2,)),
         ],

time: 65.3 us -> 61.1 us (0.936)
  Pallas kernels: 63.2 us -> 59.1 us
    pallas_call x1, Pallas kernels: 63.2 us -> 59.1 us  [per_device(): pl.pallas_call(kernel, name='convlstm', out_shape=(jax.ShapeDtypeStruct((...]
where the time goes in v4:
time: 61.1 us; the launch traced here: 61 us
  Pallas kernels  59.1 us (97%)
  local copies, waits for them, and re-layouts  1.27 us (2%)
  between operations  0.64 us (1%)
    pallas_call x1, Pallas kernels, per_device(): pl.pallas_call(kernel, name='convlstm', out_shape=(jax.ShapeDtypeStruct((...  59.1 us
    unnamed x2, local copies, waits for them, and re-layouts  1.27 us

profile of v4, /device:TPU:11, one launch (start us, length us, event | category | flops | bytes accessed | tf_op | source)
XLA Modules:
  0.0 61.0 jit_solution(10661502888776824320)
XLA Ops:
  0.6 59.1 %convlstm.1 = (bf16[2,4,4,512]{3,2,1,0:T(4,128)(2,1)S(1)}, f32[2,4,32,64]{3,2,1,0:T(8,128)S(1)}) custom-call(bf16[4,2,4,32,64]{4,3,2,1,0:T(8,128)(2,1)} %bitcast.15, bf16[2,4,32,64]{3,2,1,0:T(8,128)(2,1)} %bitcast.17, f32[2,4,32,64]{3,2,1,0:T(8,128)} %bitcast.16, f32[4,32]{1,0:T(4,128)} %gate_bias_hbm.1, f32[1,512]{1,0:T(1,128)} %bitcast.18, ...), custom_call_target="tpu_custom_call" | custom-call | tf_op jit(solution)/shard_map/convlstm/pallas_call | solution.py:571
  59.7 0.6 %copy.14 = bf16[2,4,4,512]{3,2,1,0:T(4,128)(2,1)} copy(bf16[2,4,4,512]{3,2,1,0:T(4,128)(2,1)S(1)} %get-tuple-element.8) | data formatting | bytes 65536
  60.3 0.7 %copy.15 = f32[2,4,64,32]{2,3,1,0:T(8,128)} copy(f32[2,4,64,32]{2,3,1,0:T(8,128)S(1)} %bitcast.12) | data formatting | bytes 131072

commit v5 on v4

--- a/solution.py
+++ b/solution.py
@@ -22,7 +22,7 @@
     decoded, cell_out,
     frames, hidden, cell_in, gate_bias, bias1, bias2,
     packed, packed_cell, own, edge_top, edge_bot, image, halo_top, halo_bot,
-    far_top_out, far_bot_out, far_top, far_bot, frame_top, frame_bot,
+    spread, win_out, win_in, frame_top, frame_bot,
     wi, wh, w1, w2, bias_col, cell, gin, dec_out, dec_in, cell_back,
     in_sem, w_sem, wx_send, wx_recv, s_send, s_recv, f_send, f_recv,
     x_send, x_recv, ht_send, ht_recv, hb_send, hb_recv, fin_send, fin_recv, c2_send, c2_recv, d_send, d_recv,
@@ -107,7 +107,8 @@
         copy = pltpu.make_async_copy(src, dst.at[:, :, core], w_sem.at[k])
         copy.start()
         weight_copies.append(copy)
-    for k, (src, dst) in enumerate(((w_first, w1), (w_second, w2))):
+    first_parts = [(w_first.at[:, :, :, k], w1.at[:, :, k]) for k in range(2)]
+    for k, (src, dst) in enumerate((*first_parts, (w_second, w2))):
         copy = pltpu.make_async_copy(src, dst, w_sem.at[2 + k])
         copy.start()
         weight_copies.append(copy)
@@ -128,12 +129,20 @@
     @pl.when(block == 0)
     def _():
         halo_top[...] = jnp.zeros_like(halo_top)
-        far_top[...] = jnp.zeros_like(far_top)
+        win_in[0] = jnp.zeros_like(win_in[0])
 
     @pl.when(block == 7)
     def _():
         halo_bot[...] = jnp.zeros_like(halo_bot)
-        far_bot[...] = jnp.zeros_like(far_bot)
+        win_in[2] = jnp.zeros_like(win_in[2])
+
+    lane_in = lax.broadcasted_iota(jnp.int32, (256, 512), 0)
+    lane_out = lax.broadcasted_iota(jnp.int32, (256, 512), 1)
+    row_in = lane_in // 128 + 2 * (lax.rem(lane_in, 128) // 64)
+    row_out = lax.rem(lane_out, 64) // 16
+    col_out = lane_out // 64 * 8 - 2 + lax.rem(lane_out, 16)
+    taken = (row_in == row_out) & (lax.rem(lane_in, 64) == col_out)
+    spread[...] = jnp.where(taken, 1.0, 0.0).astype(BF16)
 
     greeted = 1 + 2 * flip + 7 + jnp.where(has_up, 8, 0) + jnp.where(has_down, 8, 0)
     pl.semaphore_wait(barrier, greeted)
@@ -396,23 +405,30 @@
     lax.fori_loop(0, STEPS, step, 0)
 
     last = (STEPS + 1) % 2
-    wide = lax.broadcasted_iota(jnp.int32, (64, 128), 1) < 64
-    row_a = own[last, 0]
-    row_b = own[last, 1]
-    far_top_out[...] = jnp.where(wide, row_a, swap_halves(row_b))
-    far_bot_out[...] = jnp.where(wide, swap_halves(row_a), row_b)
+    windows = jnp.dot(own[last, 0], spread[0:128, :], preferred_element_type=F32)
+    windows = (windows + jnp.dot(own[last, 1], spread[128:256, :], preferred_element_type=F32)).astype(BF16)
+    for k in range(4):
+        low = windows[:32, k * 128 : (k + 1) * 128]
+        high = windows[32:, k * 128 : (k + 1) * 128]
+        win_out[2 * k] = jnp.where(half, low, swap_halves(high))
+        win_out[2 * k + 1] = jnp.where(half, swap_halves(low), high)
 
     @pl.when(has_up)
     def _():
-        for g in range(8):
-            send(far_top_out, far_bot.at[my_tile, :], fin_send.at[0], fin_recv.at[0], above(g))
+        for k in range(8):
+            device = above(k)
+            send(win_out.at[device[1] // 2], win_in.at[2, my_edge, :], fin_send.at[0], fin_recv.at[0], device)
 
     @pl.when(has_down)
     def _():
-        for g in range(8):
-            send(far_bot_out, far_top.at[my_tile, :], fin_send.at[1], fin_recv.at[1], below(g))
-
-    send_tiles(last, FAR_FIRST)
+        for k in range(8):
+            device = below(k)
+            send(win_out.at[device[1] // 2], win_in.at[0, my_edge, :], fin_send.at[1], fin_recv.at[1], device)
+
+    for d in FAR_FIRST:
+        device = peer(d)
+        send(win_out.at[device[1] // 2], win_in.at[1, my_edge, :], fin_send.at[2], fin_recv.at[2], device)
+    win_in[1, my_edge, :] = win_out[grp]
 
     def cell_copy(c, b):
         return pltpu.make_async_remote_copy(
@@ -432,51 +448,45 @@
         def _(c=c):
             cell_back[core] = cell[c]
 
-    weight_copies[2].wait()
-    weight_copies[3].wait()
-    wait_tiles(last)
+    for copy in weight_copies[2:]:
+        copy.wait()
+    wait_bytes(win_in.at[1, 0:224, :], fin_recv.at[2])
 
     @pl.when(has_down)
     def _():
-        wait_bytes(far_bot, fin_recv.at[0])
+        wait_bytes(win_in.at[2], fin_recv.at[0])
 
     @pl.when(has_up)
     def _():
-        wait_bytes(far_top, fin_recv.at[1])
-
-    sel_row = lax.broadcasted_iota(jnp.int32, (32, 128), 0)
-    sel_lane = lax.broadcasted_iota(jnp.int32, (32, 128), 1)
-    want = lax.rem(sel_row, 16) + grp * 8 - 2
-    chosen = (want >= 0) & (want < 64) & (sel_lane == want + 64 * (sel_row // 16))
-    pick = jnp.where(chosen, 1.0, 0.0).astype(BF16)
-
-    def window(tile):
-        return lax.dot_general(pick, tile, (((1,), (1,)), ((), ())), preferred_element_type=F32).astype(BF16)
-
-    above = window(far_top[...])
-    tile_a = window(image[last, 1])
-    tile_b = window(image[last, 2])
-    below = window(far_bot[...])
-    pixels = jnp.concatenate([above, tile_a[:16], tile_b[:16], tile_a[16:], tile_b[16:], below], axis=0)
+        wait_bytes(win_in.at[0], fin_recv.at[1])
+
+    unit = lax.broadcasted_iota(jnp.int32, (128, 128), 0) == lax.broadcasted_iota(jnp.int32, (128, 128), 1)
+    unit = jnp.where(unit, 1.0, 0.0).astype(BF16)
+
+    def window(k, first, stop):
+        turned = lax.dot_general(unit, win_in[k], (((1,), (1,)), ((), ())), preferred_element_type=F32).astype(BF16)
+        return jnp.concatenate([turned[first:stop], turned[64 + first : 64 + stop]], axis=1)
+
+    pixels = jnp.concatenate([window(0, 32, 64), window(1, 0, 64), window(2, 0, 32)], axis=0)
 
     def decode(source, rows, weight):
         parts = []
         for q in range(3):
             total = None
             for p in range(3):
-                term = jnp.dot(source[p * 16 : p * 16 + rows * 16], weight[p, q], preferred_element_type=F32)
+                term = jnp.dot(source[p * 16 : p * 16 + rows * 16], weight(p, q), preferred_element_type=F32)
                 total = term if total is None else total + term
             parts.append(total)
         return parts[1] + pltpu.roll(parts[0], 1, 0) + pltpu.roll(parts[2], rows * 16 - 1, 0)
 
-    first = decode(pixels, 6, w1) + bias1[...]
+    first = decode(pixels, 6, lambda p, q: w1[p, q].reshape(512, 512)) + bias1[...]
     first = first / (1.0 + jnp.exp(-first))
     pixel = lax.broadcasted_iota(jnp.int32, (96, 512), 0)
     image_row = block * 4 - 1 + pixel // 16
     image_col = grp * 8 - 2 + lax.rem(pixel, 16)
     inside = (image_row >= 0) & (image_row < 32) & (image_col >= 0) & (image_col < 64)
     middle = jnp.where(inside, first, 0.0).astype(BF16)
-    second = decode(middle, 4, w2) + bias2[...]
+    second = decode(middle, 4, lambda p, q: w2[p, q]) + bias2[...]
     shifted = second.reshape(4, 16, 512)
     for c in range(2):
         dec_out[c] = shifted[:, 2 + 4 * c : 6 + 4 * c, :].astype(BF16)
@@ -517,15 +527,15 @@
         wait_bytes(image.at[2 + t, 1, 0:256, :], f_send.at[2, t])
         wait_edges_sent(2 + t)
     wait_sent(1 - last)
-    wait_bytes(image.at[last, 1:3, 0:448, :], x_send.at[last])
+    wait_bytes(win_in.at[1, 0:224, :], fin_send.at[2])
 
     @pl.when(has_up)
     def _():
-        wait_bytes(far_top, fin_send.at[0])
+        wait_bytes(win_in.at[0], fin_send.at[0])
 
     @pl.when(has_down)
     def _():
-        wait_bytes(far_bot, fin_send.at[1])
+        wait_bytes(win_in.at[2], fin_send.at[1])
 
     for copy in trades:
         copy.wait_send()
@@ -565,7 +575,7 @@
         second_bias.reshape(1, -1),
         gate_rows(input_weight),
         gate_rows(hidden_weight),
-        first_weight,
+        first_weight.reshape(3, 3, 8, 2, 32, 512),
         second_weight,
     )
     decoded, cell = pl.pallas_call(
@@ -592,15 +602,14 @@
             pltpu.VMEM((slots, 4, 512, 128), BF16),
             pltpu.VMEM((slots, 256, 128), BF16),
             pltpu.VMEM((slots, 256, 128), BF16),
-            pltpu.VMEM((64, 128), BF16),
-            pltpu.VMEM((64, 128), BF16),
-            pltpu.VMEM((512, 128), BF16),
-            pltpu.VMEM((512, 128), BF16),
+            pltpu.VMEM((256, 512), BF16),
+            pltpu.VMEM((8, 32, 128), BF16),
+            pltpu.VMEM((3, 256, 128), BF16),
             pltpu.VMEM((STEPS, 256, 128), BF16),
             pltpu.VMEM((STEPS, 256, 128), BF16),
             pltpu.VMEM((3, 3, 2, 128, 512), BF16),
             pltpu.VMEM((3, 3, 2, 128, 512), BF16),
-            pltpu.VMEM((3, 3, 512, 512), BF16),
+            pltpu.VMEM((3, 3, 2, 8, 32, 512), BF16),
             pltpu.VMEM((3, 3, 512, 512), BF16),
             pltpu.VMEM((2, 128, 128), F32),
             pltpu.VMEM((2, 32, 256), F32),
@@ -608,9 +617,9 @@
             pltpu.VMEM((2, 4, 4, 512), BF16),
             pltpu.VMEM((2, 4, 4, 512), BF16),
             pltpu.VMEM((2, 32, 256), F32),
-            dma((6,)), dma((4,)), dma((3,)), dma((3,)), dma((3, 2)), dma((3, 2)), dma((3, STEPS)), dma((3, STEPS)),
+            dma((6,)), dma((5,)), dma((3,)), dma((3,)), dma((3, 2)), dma((3, 2)), dma((3, STEPS)), dma((3, STEPS)),
             dma((slots,)), dma((slots,)), dma((slots,)), dma((slots,)), dma((slots,)), dma((slots,)),
-            dma((2,)), dma((2,)), dma((2,)), dma((2,)), dma((2,)), dma((2,)),
+            dma((3,)), dma((3,)), dma((2,)), dma((2,)), dma((2,)), dma((2,)),
         ],
         compiler_params=pltpu.CompilerParams(
             collective_id=0, has_side_effects=True, vmem_limit_bytes=50 << 20

time: 61.1 us -> 59.8 us (0.979)
  Pallas kernels: 59.1 us -> 57.8 us
    pallas_call x1, Pallas kernels: 59.1 us -> 57.8 us  [per_device(): pl.pallas_call(kernel, name='convlstm', out_shape=(jax.ShapeDtypeStruct((...]
where the time goes in v5:
time: 59.8 us; the launch traced here: 59.7 us
  Pallas kernels  57.8 us (97%)
  local copies, waits for them, and re-layouts  1.27 us (2%)
  between operations  0.64 us (1%)
    pallas_call x1, Pallas kernels, per_device(): pl.pallas_call(kernel, name='convlstm', out_shape=(jax.ShapeDtypeStruct((...  57.8 us
    unnamed x2, local copies, waits for them, and re-layouts  1.27 us

profile of v5, /device:TPU:11, one launch (start us, length us, event | category | flops | bytes accessed | tf_op | source)
XLA Modules:
  0.0 59.7 jit_solution(15698841712625773253)
XLA Ops:
  0.6 57.8 %convlstm.1 = (bf16[2,4,4,512]{3,2,1,0:T(4,128)(2,1)S(1)}, f32[2,4,32,64]{3,2,1,0:T(8,128)S(1)}) custom-call(bf16[4,2,4,32,64]{4,3,2,1,0:T(8,128)(2,1)} %bitcast.17, bf16[2,4,32,64]{3,2,1,0:T(8,128)(2,1)} %bitcast.19, f32[2,4,32,64]{3,2,1,0:T(8,128)} %bitcast.18, f32[4,32]{1,0:T(4,128)} %gate_bias_hbm.1, f32[1,512]{1,0:T(1,128)} %bitcast.20, ...), custom_call_target="tpu_custom_call" | custom-call | tf_op jit(solution)/shard_map/convlstm/pallas_call | solution.py:581
  58.5 0.6 %copy.14 = bf16[2,4,4,512]{3,2,1,0:T(4,128)(2,1)} copy(bf16[2,4,4,512]{3,2,1,0:T(4,128)(2,1)S(1)} %get-tuple-element.8) | data formatting | bytes 65536
  59.1 0.7 %copy.15 = f32[2,4,64,32]{2,3,1,0:T(8,128)} copy(f32[2,4,64,32]{2,3,1,0:T(8,128)S(1)} %bitcast.13) | data formatting | bytes 131072

commit v6 on v5

--- a/solution.py
+++ b/solution.py
@@ -196,8 +196,6 @@
         weight_trade(1, w_hid, wh.at[:, :, core]),
         weight_trade(2, bias_col.at[core], bias_col.at[core]),
     ]
-    for copy in trades:
-        copy.start()
     wait_trades((0,))
 
     half = lax.broadcasted_iota(jnp.int32, (32, 128), 1) < 64
@@ -340,6 +338,8 @@
     broadcast(1)
     send_edges(2)
     start_trades((1, 2))
+    for copy in trades:
+        copy.start()
     frame_second(0)
     wait_trades((1, 2))
     frame_first(1)
@@ -552,6 +552,17 @@
             dec_copy(b, core).wait_send()
 
         decoded[b] = dec_in[b]
+
+
+def give_out(decoded, cell, decoded_out, cell_out, sem):
+    copies = [
+        pltpu.make_async_copy(decoded, decoded_out, sem.at[0]),
+        pltpu.make_async_copy(cell, cell_out, sem.at[1]),
+    ]
+    for copy in copies:
+        copy.start()
+    for copy in copies:
+        copy.wait()
 
 
 def per_device(
@@ -627,6 +638,18 @@
     )(
         *(pltpu.with_memory_space_constraint(array, pltpu.HBM) for array in operands)
     )
+    decoded, cell = pl.pallas_call(
+        give_out,
+        name="give_out",
+        out_shape=(
+            jax.ShapeDtypeStruct((2, 4, 4, 512), BF16),
+            jax.ShapeDtypeStruct((2, 4, 32, 64), F32),
+        ),
+        in_specs=[vmem, vmem],
+        out_specs=(hbm, hbm),
+        scratch_shapes=[dma((2,))],
+        compiler_params=pltpu.CompilerParams(vmem_limit_bytes=1 << 20),
+    )(decoded, cell)
     return decoded, cell.transpose(0, 1, 3, 2)
 
 

time: 59.8 us -> 59.3 us (level)
  local copies, waits for them, and re-layouts: 1.27 us -> 0 us
  Pallas kernels: 57.8 us -> 58.5 us
    unnamed x2 -> x0, local copies, waits for them, and re-layouts: 1.27 us -> none
    pallas_call x0 -> x1, Pallas kernels: none -> 0.69 us  [per_device(): pl.pallas_call(give_out, name='give_out', out_shape=(jax.ShapeDtypeStruct...]
where the time goes in v6:
time: 59.3 us; the launch traced here: 59.1 us
  Pallas kernels  58.5 us (99%)
  between operations  0.64 us (1%)
    pallas_call x1, Pallas kernels, per_device(): pl.pallas_call(kernel, name='convlstm', out_shape=(jax.ShapeDtypeStruct((...  57.8 us

profile of v6, /device:TPU:11, one launch (start us, length us, event | category | flops | bytes accessed | tf_op | source)
XLA Modules:
  0.0 59.1 jit_solution(18341947596110608984)
XLA Ops:
  0.6 57.8 %convlstm.1 = (bf16[2,4,4,512]{3,2,1,0:T(4,128)(2,1)S(1)}, f32[2,4,32,64]{3,2,1,0:T(8,128)S(1)}) custom-call(bf16[4,2,4,32,64]{4,3,2,1,0:T(8,128)(2,1)} %bitcast.16, bf16[2,4,32,64]{3,2,1,0:T(8,128)(2,1)} %bitcast.18, f32[2,4,32,64]{3,2,1,0:T(8,128)} %bitcast.17, f32[4,32]{1,0:T(4,128)} %gate_bias_hbm.1, f32[1,512]{1,0:T(1,128)} %bitcast.19, ...), custom_call_target="tpu_custom_call" | custom-call | tf_op jit(solution)/shard_map/convlstm/pallas_call | solution.py:592
  58.5 0.7 %give_out.1 = (bf16[2,4,4,512]{3,2,1,0:T(4,128)(2,1)}, f32[2,4,32,64]{3,2,1,0:T(8,128)}) custom-call(bf16[2,4,4,512]{3,2,1,0:T(4,128)(2,1)S(1)} %get-tuple-element.6.decoded, f32[2,4,32,64]{3,2,1,0:T(8,128)S(1)} %get-tuple-element.7.cell), custom_call_target="tpu_custom_call" | custom-call | tf_op jit(solution)/shard_map/give_out/pallas_call | solution.py:641

commit v7 on v6

--- a/solution.py
+++ b/solution.py
@@ -82,25 +82,25 @@
     def greet(device):
         pl.semaphore_signal(barrier, inc=1, device_id=device, device_id_type=MESH)
 
+    @pl.when(has_up)
+    def _():
+        for g in range(8):
+            greet(above(g))
+
+    @pl.when(has_down)
+    def _():
+        for g in range(8):
+            greet(below(g))
+
+    for d in FAR_FIRST:
+        greet(peer(d))
+
     greet(sibling)
 
     @pl.when(flip == 1)
     def _():
         greet(trade(0))
         greet(trade(1))
-
-    for d in FAR_FIRST:
-        greet(peer(d))
-
-    @pl.when(has_up)
-    def _():
-        for g in range(8):
-            greet(above(g))
-
-    @pl.when(has_down)
-    def _():
-        for g in range(8):
-            greet(below(g))
 
     weight_copies = []
     for k, (src, dst) in enumerate(((w_in, wi), (w_hid, wh))):

time: 59.3 us -> 59.2 us (level)
  no operation moved by 1% of the time
where the time goes in v7:
time: 59.2 us; the launch traced here: 59.1 us
  Pallas kernels  58.4 us (99%)
  between operations  0.64 us (1%)
    pallas_call x1, Pallas kernels, per_device(): pl.pallas_call(kernel, name='convlstm', out_shape=(jax.ShapeDtypeStruct((...  57.7 us

profile of v7, /device:TPU:11, one launch (start us, length us, event | category | flops | bytes accessed | tf_op | source)
XLA Modules:
  0.0 59.1 jit_solution(8044165964665956295)
XLA Ops:
  0.6 57.7 %convlstm.1 = (bf16[2,4,4,512]{3,2,1,0:T(4,128)(2,1)S(1)}, f32[2,4,32,64]{3,2,1,0:T(8,128)S(1)}) custom-call(bf16[4,2,4,32,64]{4,3,2,1,0:T(8,128)(2,1)} %bitcast.16, bf16[2,4,32,64]{3,2,1,0:T(8,128)(2,1)} %bitcast.18, f32[2,4,32,64]{3,2,1,0:T(8,128)} %bitcast.17, f32[4,32]{1,0:T(4,128)} %gate_bias_hbm.1, f32[1,512]{1,0:T(1,128)} %bitcast.19, ...), custom_call_target="tpu_custom_call" | custom-call | tf_op jit(solution)/shard_map/convlstm/pallas_call | solution.py:592
  58.4 0.7 %give_out.1 = (bf16[2,4,4,512]{3,2,1,0:T(4,128)(2,1)}, f32[2,4,32,64]{3,2,1,0:T(8,128)}) custom-call(bf16[2,4,4,512]{3,2,1,0:T(4,128)(2,1)S(1)} %get-tuple-element.6.decoded, f32[2,4,32,64]{3,2,1,0:T(8,128)S(1)} %get-tuple-element.7.cell), custom_call_target="tpu_custom_call" | custom-call | tf_op jit(solution)/shard_map/give_out/pallas_call | solution.py:641

commit v8 on v7

--- a/solution.py
+++ b/solution.py
@@ -430,6 +430,18 @@
         send(win_out.at[device[1] // 2], win_in.at[1, my_edge, :], fin_send.at[2], fin_recv.at[2], device)
     win_in[1, my_edge, :] = win_out[grp]
 
+    for copy in weight_copies[2:]:
+        copy.wait()
+    wait_bytes(win_in.at[1, 0:224, :], fin_recv.at[2])
+
+    @pl.when(has_down)
+    def _():
+        wait_bytes(win_in.at[2], fin_recv.at[0])
+
+    @pl.when(has_up)
+    def _():
+        wait_bytes(win_in.at[0], fin_recv.at[1])
+
     def cell_copy(c, b):
         return pltpu.make_async_remote_copy(
             src_ref=cell.at[c], dst_ref=cell_back.at[b],
@@ -447,18 +459,6 @@
         @pl.when(stays)
         def _(c=c):
             cell_back[core] = cell[c]
-
-    for copy in weight_copies[2:]:
-        copy.wait()
-    wait_bytes(win_in.at[1, 0:224, :], fin_recv.at[2])
-
-    @pl.when(has_down)
-    def _():
-        wait_bytes(win_in.at[2], fin_recv.at[0])
-
-    @pl.when(has_up)
-    def _():
-        wait_bytes(win_in.at[0], fin_recv.at[1])
 
     unit = lax.broadcasted_iota(jnp.int32, (128, 128), 0) == lax.broadcasted_iota(jnp.int32, (128, 128), 1)
     unit = jnp.where(unit, 1.0, 0.0).astype(BF16)

time: 59.2 us -> 59.2 us (level)
  no operation moved by 1% of the time
where the time goes in v8:
time: 59.2 us; the launch traced here: 59.1 us
  Pallas kernels  58.4 us (99%)
  between operations  0.64 us (1%)
    pallas_call x1, Pallas kernels, per_device(): pl.pallas_call(kernel, name='convlstm', out_shape=(jax.ShapeDtypeStruct((...  57.8 us

profile of v8, /device:TPU:11, one launch (start us, length us, event | category | flops | bytes accessed | tf_op | source)
XLA Modules:
  0.0 59.1 jit_solution(16454669312983776371)
XLA Ops:
  0.6 57.8 %convlstm.1 = (bf16[2,4,4,512]{3,2,1,0:T(4,128)(2,1)S(1)}, f32[2,4,32,64]{3,2,1,0:T(8,128)S(1)}) custom-call(bf16[4,2,4,32,64]{4,3,2,1,0:T(8,128)(2,1)} %bitcast.16, bf16[2,4,32,64]{3,2,1,0:T(8,128)(2,1)} %bitcast.18, f32[2,4,32,64]{3,2,1,0:T(8,128)} %bitcast.17, f32[4,32]{1,0:T(4,128)} %gate_bias_hbm.1, f32[1,512]{1,0:T(1,128)} %bitcast.19, ...), custom_call_target="tpu_custom_call" | custom-call | tf_op jit(solution)/shard_map/convlstm/pallas_call | solution.py:592
  58.4 0.7 %give_out.1 = (bf16[2,4,4,512]{3,2,1,0:T(4,128)(2,1)}, f32[2,4,32,64]{3,2,1,0:T(8,128)}) custom-call(bf16[2,4,4,512]{3,2,1,0:T(4,128)(2,1)S(1)} %get-tuple-element.6.decoded, f32[2,4,32,64]{3,2,1,0:T(8,128)S(1)} %get-tuple-element.7.cell), custom_call_target="tpu_custom_call" | custom-call | tf_op jit(solution)/shard_map/give_out/pallas_call | solution.py:641
